TPU v7x, 32 devices: a whole 2x2x4 slice. The times are simulated.
32 devices in a mesh: fsdp: 8 (over y, x, core), dp: 4 (over z).
Axes of the slice: x: 2, y: 2, z: 4, core: 2. Of those that a mesh axis runs over, the one named last changes fastest.
Arguments:
- hidden_in: bfloat16 [17408, 1024], P(('fsdp', 'dp')), may hold values from -6 to 6
- cotangent: bfloat16 [17408, 1024], P(('fsdp', 'dp')), may hold values from -6 to 6
- segment_ids: int32 [32, 544], P(('fsdp', 'dp')), may hold values from 0 to 7, never falling along the last dimension, each value on 1 to 128 neighbouring positions
- box_left: int32 [32, 544], P(('fsdp', 'dp')), may hold values from 0 to 63
- box_top: int32 [32, 544], P(('fsdp', 'dp')), may hold values from 0 to 63
- query_weight: bfloat16 [1024, 1024], P('fsdp'), may hold values from -0.1875 to 0.1875
- query_bias: bfloat16 [1024], P('fsdp'), may hold values from -3 to 3
- key_weight: bfloat16 [1024, 1024], P('fsdp'), may hold values from -0.1875 to 0.1875
- value_weight: bfloat16 [1024, 1024], P('fsdp'), may hold values from -0.1875 to 0.1875
- value_bias: bfloat16 [1024], P('fsdp'), may hold values from -3 to 3
- output_weight: bfloat16 [1024, 1024], P('fsdp'), may hold values from -0.75 to 0.75
- output_bias: bfloat16 [1024], P('fsdp'), may hold values from -2 to 2
- first_gain: bfloat16 [1024], P('fsdp'), may hold values from 0.25 to 1.75
- first_shift: bfloat16 [1024], P('fsdp'), may hold values from -2 to 2
- inner_weight: bfloat16 [1024, 4096], P('fsdp'), may hold values from -0.1875 to 0.1875
- inner_bias: bfloat16 [4096], P('fsdp'), may hold values from -3 to 3
- outer_weight: bfloat16 [4096, 1024], P('fsdp'), may hold values from -0.125 to 0.125
- outer_bias: bfloat16 [1024], P('fsdp'), may hold values from -2 to 2
- second_gain: bfloat16 [1024], P('fsdp'), may hold values from 0.25 to 1.75
- second_shift: bfloat16 [1024], P('fsdp'), may hold values from -2 to 2
- bucket_table: bfloat16 [6144], P('fsdp'), may hold values from -5 to 5
Outputs:
- layer_out: bfloat16 [17408, 1024], P(('fsdp', 'dp'))
- input_grad: float32 [17408, 1024], P(('fsdp', 'dp'))
- query_weight_grad: float32 [1024, 1024], P('fsdp')
- query_bias_grad: float32 [1024], P('fsdp')
- key_weight_grad: float32 [1024, 1024], P('fsdp')
- value_weight_grad: float32 [1024, 1024], P('fsdp')
- value_bias_grad: float32 [1024], P('fsdp')
- output_weight_grad: float32 [1024, 1024], P('fsdp')
- output_bias_grad: float32 [1024], P('fsdp')
- first_gain_grad: float32 [1024], P('fsdp')
- first_shift_grad: float32 [1024], P('fsdp')
- inner_weight_grad: float32 [1024, 4096], P('fsdp')
- inner_bias_grad: float32 [4096], P('fsdp')
- outer_weight_grad: float32 [4096, 1024], P('fsdp')
- outer_bias_grad: float32 [1024], P('fsdp')
- second_gain_grad: float32 [1024], P('fsdp')
- second_shift_grad: float32 [1024], P('fsdp')
- bucket_table_grad: float32 [6144], P('fsdp')
Inputs may be any that keep to these rules, and one draw needn't show every extreme that they name: `segment_ids`: within each packed row page numbers never fall, each page holds 1 to 128 slots, and one page of the row holds exactly 128.
All inputs are finite; a program needn't handle non-finite values.
Results may differ from a plain program's by a relative error of at most 0.017.
Values may be sent and summed in bfloat16 or wider, within the bound.
No kernel may reach another device: no remote copies, remote signals or barrier semaphores. Data moves between devices by JAX's collectives and lax.ppermute only.
A program may use at most 256 MiB of HBM per device.

v0:
```python
from functools import partial

import jax
import jax.numpy as jnp
import numpy as np
from jax import lax
from jax.experimental import pallas as pl
from jax.experimental.pallas import tpu as pltpu
from jax.sharding import PartitionSpec as P

HEADS = 16
HEAD_DIM = 64
PAIRS = HEADS // 2
NB = 128
PAGE = 128
PAGES = 8
EPSILON = 1e-05
BLOCKED = -1e30
BF = jnp.bfloat16
F32 = jnp.float32
VMEM_LIMIT = 62 * 1024 * 1024
SCALE = 0.3


def cost(microseconds):
    return pl.CostEstimate(
        flops=1 + int(microseconds * SCALE * 1e9), bytes_accessed=1, transcendentals=0
    )


NT = (((1,), (1,)), ((), ()))
TN = (((0,), (0,)), ((), ()))


def dot(left_side, right_side, dims=(((1,), (0,)), ((), ()))):
    return lax.dot_general(left_side, right_side, dims, preferred_element_type=F32)


def flips(bit_of):
    return [(i, i ^ bit_of(i & 1)) for i in range(8)]


NEAR = flips(lambda c: 2 if c else 4)
FAR = flips(lambda c: 4 if c else 2)
TWIN = flips(lambda c: 1)


def block_order(me):
    rel0 = np.array([0, 4, 2, 6, 1, 3, 5, 7], np.int32)
    rel1 = np.array([0, 2, 4, 6, 1, 5, 3, 7], np.int32)
    rel = jnp.where((me & 1) == 0, rel0, rel1)
    return jnp.bitwise_xor(me, rel).astype(jnp.int32)


def hop(value, pairs):
    return lax.ppermute(value, "fsdp", pairs)


def after(value, *others):
    return lax.optimization_barrier((value,) + others)[0]


def fold_far(stay, other):
    return stay[0] + other[0], stay[1] + other[1]


def trade(value, bit):
    return lax.ppermute(value, "dp", [(i, i ^ bit) for i in range(4)])


def cut(value, bit):
    high = (lax.axis_index("dp") & bit) // bit
    halves = value.reshape((2, value.shape[0] // 2) + value.shape[1:])
    return (
        lax.dynamic_index_in_dim(halves, high, 0, keepdims=False),
        lax.dynamic_index_in_dim(halves, 1 - high, 0, keepdims=False),
    )


def paste(mine, other, bit):
    high = (lax.axis_index("dp") & bit) != 0
    return jnp.concatenate([jnp.where(high, other, mine), jnp.where(high, mine, other)], axis=0)


def pack_kernel(shapes, *refs):
    items, out_ref, sem = refs[: len(shapes) + 3], refs[-2], refs[-1]
    rows = items[0].shape[0]
    copies = [
        pltpu.make_async_copy(items[j], out_ref.at[pl.ds(j * rows, rows), :], sem.at[j])
        for j in range(3)
    ]
    for copy in copies:
        copy.start()
    spot = 0
    out_ref[3 * rows :, :] = jnp.zeros((16, out_ref.shape[1]), BF)
    for item, count in zip(items[3:], shapes):
        for i in range(count):
            row, lane = 3 * rows + spot // 8, spot % 8 * 128
            out_ref[row : row + 1, lane : lane + 128] = item[i : i + 1, :]
            spot += 1
    for copy in copies:
        copy.wait()


def pack(weights, vectors):
    rows, columns = weights[0].shape
    vectors = [item.reshape(-1, 128) for item in vectors]
    return pl.pallas_call(
        partial(pack_kernel, tuple(item.shape[0] for item in vectors)),
        out_shape=jax.ShapeDtypeStruct((3 * rows + 16, columns), BF),
        in_specs=[pl.BlockSpec(memory_space=pltpu.HBM)] * 3
        + [pl.BlockSpec(memory_space=pltpu.VMEM)] * len(vectors),
        out_specs=pl.BlockSpec(memory_space=pltpu.VMEM),
        scratch_shapes=[pltpu.SemaphoreType.DMA((3,))],
        cost_estimate=cost(3),
    )(*weights, *vectors)


def emit(found, k, others, outs):
    if others:
        outs[k // 2][k % 2] = (found + others[k][...].astype(F32)).astype(BF)
    else:
        outs[k][...] = found.astype(BF)


def turned_kernel(fold, order_ref, left_ref, right_ref, *refs):
    others, outs, turned = refs[: 4 * fold], refs[4 * fold : -1], refs[-1]
    i = pl.program_id(0)

    @pl.when(i == 0)
    def _():
        turned[...] = right_ref[...].T

    found = dot(turned[...], left_ref[...])
    for k in range(4):

        @pl.when(i == k)
        def _():
            emit(found, k, others, outs)


def turned_blocks(order, first, left, right, others=()):
    depth, rows, columns = left.shape[0], left.shape[1] // 8, right.shape[1]
    fold = int(bool(others))
    whole = pl.BlockSpec((columns, rows), lambda i, n: (0, 0))
    if fold:
        out_specs = (pl.BlockSpec((2, columns, rows), lambda i, n: (0, 0, 0)),) * 2
        shapes = (jax.ShapeDtypeStruct((2, columns, rows), BF),) * 2
    else:
        out_specs = (whole,) * 4
        shapes = (jax.ShapeDtypeStruct((columns, rows), BF),) * 4
    return pl.pallas_call(
        partial(turned_kernel, fold),
        grid_spec=pltpu.PrefetchScalarGridSpec(
            num_scalar_prefetch=1,
            grid=(4,),
            in_specs=[
                pl.BlockSpec((depth, rows), lambda i, n: (0, n[first + i])),
                pl.BlockSpec((depth, columns), lambda i, n: (0, 0)),
            ]
            + [whole] * (4 * fold),
            out_specs=out_specs,
            scratch_shapes=[pltpu.VMEM((columns, depth), left.dtype)],
        ),
        out_shape=shapes,
        compiler_params=pltpu.CompilerParams(vmem_limit_bytes=VMEM_LIMIT),
        cost_estimate=cost(7),
    )(order, left, right, *others)


def grad_kernel(first, counts, fold, order_ref, *refs):
    pieces = len(counts)
    lefts, rights = refs[:pieces], refs[pieces : 2 * pieces]
    others = refs[2 * pieces : 2 * pieces + 4 * fold]
    outs, turned = refs[2 * pieces + 4 * fold : -pieces], refs[-pieces:]
    i = pl.program_id(0)
    rows = turned[0].shape[0] // 4
    start = 0
    for left_ref, right_ref, kept, count in zip(lefts, rights, turned, counts):

        @pl.when(i == start)
        def _():
            for k in range(4):
                kept[k * rows : (k + 1) * rows, :] = left_ref[
                    :, lanes(order_ref, first + k, rows)
                ].T

        @pl.when((i >= start) & (i < start + count))
        def _():
            found = dot(kept[...], right_ref[...])
            for k in range(4):
                emit(found[k * rows : (k + 1) * rows], k, others, outs)

        start += count


def grad_blocks(order, first, pairs, tile, others=()):
    rows = pairs[0][0].shape[1] // 8
    counts = [right.shape[1] // tile for _, right in pairs]
    total = sum(counts)
    fold = int(bool(others))
    in_specs = [pl.BlockSpec(left.shape, lambda i, n: (0, 0)) for left, _ in pairs]
    start = 0
    for (_, right), count in zip(pairs, counts):

        def at(i, n, start=start, count=count):
            return 0, jnp.clip(i - start, 0, count - 1)

        in_specs.append(pl.BlockSpec((right.shape[0], tile), at))
        start += count
    one = pl.BlockSpec((rows, tile), lambda i, n: (0, i))
    if fold:
        out_specs = (pl.BlockSpec((2, rows, tile), lambda i, n: (0, 0, i)),) * 2
        shapes = (jax.ShapeDtypeStruct((2, rows, total * tile), BF),) * 2
    else:
        out_specs = (one,) * 4
        shapes = (jax.ShapeDtypeStruct((rows, total * tile), BF),) * 4
    return pl.pallas_call(
        partial(grad_kernel, first, tuple(counts), fold),
        grid_spec=pltpu.PrefetchScalarGridSpec(
            num_scalar_prefetch=1,
            grid=(total,),
            in_specs=in_specs + [one] * (4 * fold),
            out_specs=out_specs,
            scratch_shapes=[pltpu.VMEM((4 * rows, left.shape[0]), BF) for left, _ in pairs],
        ),
        out_shape=shapes,
        compiler_params=pltpu.CompilerParams(vmem_limit_bytes=VMEM_LIMIT),
        cost_estimate=cost(2 * total),
    )(
        order,
        *[left for left, _ in pairs],
        *[right for _, right in pairs],
        *others,
    )


def to_twin(blocks):
    return [hop(block, TWIN) for block in blocks]


def lanes(order_ref, k, size):
    return pl.ds(pl.multiple_of(order_ref[k] * size, size), size)


def one_hot(shape, test):
    row = lax.broadcasted_iota(jnp.int32, shape, 0)
    lane = lax.broadcasted_iota(jnp.int32, shape, 1)
    return test(row, lane)


def precise(left_side, right_side, dims=(((1,), (0,)), ((), ()))):
    return lax.dot_general(
        left_side, right_side, dims, precision=lax.Precision.HIGHEST, preferred_element_type=F32
    )


def tables_kernel(table_ref, lookup_ref, slide_ref, flat):
    for i in range(48):
        flat[i : i + 1, :] = table_ref[i]
    wide = one_hot((NB, 16), lambda r, c: r // 8 == c).astype(F32)
    mine = one_hot((NB, NB), lambda r, c: c // 16 == r % 8)
    heads = one_hot((HEADS, NB), lambda r, c: c % 16 == r).astype(F32)
    by_head = []
    for kind in range(3):
        rows = jnp.where(mine, precise(wide, flat[16 * kind : 16 * (kind + 1), :]), 0.0)
        by_head.append(precise(heads, rows, NT))
    spot = one_hot(
        (2 * PAGE, NB),
        lambda m, bucket: jnp.clip(jnp.where(m <= PAGE, -m, 2 * PAGE - m), -64, 63) + 64 == bucket,
    ).astype(F32)
    position = precise(by_head[0], spot, NT)
    left_all = pltpu.roll(by_head[1], 64, 1)
    top_all = pltpu.roll(by_head[2], 64, 1)
    same = one_hot((NB, NB), lambda r, c: (r < 64) == (c < 64))
    for head in range(HEADS):
        base = jnp.broadcast_to(position[head : head + 1, :], (PAGE, 2 * PAGE))
        slid = pltpu.roll(base, 0, 1, stride=1, stride_axis=0)
        half = (head % 2) * PAGE
        slide_ref[head // 2, :, half : half + PAGE] = slid[:, :PAGE]
        left = jnp.broadcast_to(left_all[head : head + 1, :], (64, NB))
        top = jnp.broadcast_to(top_all[head : head + 1, :], (64, NB))
        slid = pltpu.roll(
            jnp.concatenate([left, top], axis=0), 0, 1, stride=1, stride_axis=0
        )
        lookup_ref[:, head * NB : (head + 1) * NB] = jnp.where(same, slid, 0.0).astype(BF)


def make_tables(table):
    return pl.pallas_call(
        tables_kernel,
        out_shape=(
            jax.ShapeDtypeStruct((NB, HEADS * NB), BF),
            jax.ShapeDtypeStruct((PAIRS, PAGE, 2 * PAGE), F32),
        ),
        scratch_shapes=[pltpu.VMEM((48, NB), F32)],
        compiler_params=pltpu.CompilerParams(vmem_limit_bytes=VMEM_LIMIT),
        cost_estimate=cost(3),
    )(table)


def split_heads(tile):
    lane = lax.broadcasted_iota(jnp.int32, tile.shape, 1)
    zero = jnp.zeros_like(tile)
    return jnp.concatenate(
        [jnp.where(lane < HEAD_DIM, tile, zero), jnp.where(lane >= HEAD_DIM, tile, zero)],
        axis=0,
    )


def join_heads(tall):
    lane = lax.broadcasted_iota(jnp.int32, (PAGE, NB), 1)
    return jnp.where(lane < HEAD_DIM, tall[:PAGE, :NB], tall[PAGE:, :NB])


def attend_kernel(
    length_ref, q_ref, k_ref, v_ref, box_ref, lookup_ref, slide_ref, context_ref, prob_ref, logit
):
    length = length_ref[pl.program_id(0)]
    inside = lax.broadcasted_iota(jnp.int32, (PAGE, 2 * PAGE), 0) < length
    boxes = box_ref[...]
    for pair in range(PAIRS):
        at = slice(pair * NB, (pair + 1) * NB)
        looked = dot(boxes, lookup_ref[:, 2 * pair * NB : 2 * (pair + 1) * NB]).astype(BF)
        looked = jnp.concatenate([looked[:, :NB], looked[:, NB:]], axis=0)
        asked = jnp.concatenate([split_heads(q_ref[:, at]), looked], axis=1)
        offered = jnp.concatenate([k_ref[:, at], boxes], axis=1)
        logit[pair] = dot(offered, asked, NT)
    for pair in range(PAIRS):
        logits = jnp.where(inside, logit[pair] + slide_ref[pair], BLOCKED)
        peak = jnp.max(logits, axis=0, keepdims=True)
        grown = jnp.exp(logits - peak)
        total = jnp.sum(grown, axis=0, keepdims=True)
        prob_ref[0, pair] = (grown * (1.0 / total)).astype(BF)
    for pair in range(PAIRS):
        at = slice(pair * NB, (pair + 1) * NB)
        context_ref[:, at] = join_heads(dot(prob_ref[0, pair], v_ref[:, at], TN)).astype(BF)


def attend(lengths, queries, keys, values, boxes, lookup, slide):
    wide = pl.BlockSpec((PAGE, HEADS * HEAD_DIM), lambda i, n: (i, 0))
    return pl.pallas_call(
        attend_kernel,
        grid_spec=pltpu.PrefetchScalarGridSpec(
            num_scalar_prefetch=1,
            grid=(PAGES,),
            in_specs=[
                wide,
                wide,
                wide,
                pl.BlockSpec((PAGE, NB), lambda i, n: (i, 0)),
                pl.BlockSpec((NB, HEADS * NB), lambda i, n: (0, 0)),
                pl.BlockSpec((PAIRS, PAGE, 2 * PAGE), lambda i, n: (0, 0, 0)),
            ],
            out_specs=(
                wide,
                pl.BlockSpec((1, PAIRS, PAGE, 2 * PAGE), lambda i, n: (i, 0, 0, 0)),
            ),
            scratch_shapes=[pltpu.VMEM((PAIRS, PAGE, 2 * PAGE), F32)],
        ),
        out_shape=(
            jax.ShapeDtypeStruct((PAGES * PAGE, HEADS * HEAD_DIM), BF),
            jax.ShapeDtypeStruct((PAGES, PAIRS, PAGE, 2 * PAGE), BF),
        ),
        compiler_params=pltpu.CompilerParams(vmem_limit_bytes=VMEM_LIMIT),
        cost_estimate=cost(13.5),
    )(lengths, queries, keys, values, boxes, lookup, slide)


def attend_back_kernel(
    q_ref,
    k_ref,
    v_ref,
    g_ref,
    box_ref,
    flip_ref,
    prob_ref,
    grad_ref,
    slide_sum_ref,
    box_sum_ref,
    bias_sum_ref,
    slide_acc,
    box_acc,
    d_prob,
    d_logit,
    boxed,
):
    page = pl.program_id(0)

    @pl.when(page == 0)
    def _():
        slide_acc[...] = jnp.zeros_like(slide_acc)
        box_acc[...] = jnp.zeros_like(box_acc)
        bias_sum_ref[...] = jnp.zeros_like(bias_sum_ref)

    boxes = box_ref[...]
    width = HEADS * HEAD_DIM
    scale = HEAD_DIM ** (-0.5)
    for pair in range(PAIRS):
        at = slice(pair * NB, (pair + 1) * NB)
        pulled = split_heads(g_ref[:, at])
        d_prob[pair] = dot(v_ref[:, at], pulled, NT)
        grad_ref[:, 2 * width + pair * NB : 2 * width + (pair + 1) * NB] = dot(
            prob_ref[0, pair], pulled
        ).astype(BF)
    for pair in range(PAIRS):
        prob = prob_ref[0, pair].astype(F32)
        inner = jnp.sum(prob * d_prob[pair], axis=0, keepdims=True)
        found = prob * (d_prob[pair] - inner)
        slide_acc[pair] += found
        d_logit[pair] = found.astype(BF)
    for pair in range(PAIRS):
        at = slice(pair * NB, (pair + 1) * NB)
        offered = jnp.concatenate([k_ref[:, at], boxes], axis=1)
        back = dot(d_logit[pair], offered, TN)
        grad_ref[:, at] = (join_heads(back) * scale).astype(BF)
        grad_ref[:, width + pair * NB : width + (pair + 1) * NB] = dot(
            d_logit[pair], split_heads(q_ref[:, at])
        ).astype(BF)
        tall = back[:, NB:].astype(BF)
        boxed[:, 2 * pair * NB : 2 * (pair + 1) * NB] = jnp.concatenate(
            [tall[:PAGE], tall[PAGE:]], axis=1
        )
    box_acc[...] += dot(flip_ref[...], boxed[...])
    for part in range(3 * width // 512):
        at = slice(part * 512, (part + 1) * 512)
        bias_sum_ref[:, at] += fold_rows(grad_ref[:, at].astype(F32))

    @pl.when(page == PAGES - 1)
    def _():
        row = lax.broadcasted_iota(jnp.int32, (NB, NB), 0)
        lane = lax.broadcasted_iota(jnp.int32, (NB, NB), 1)
        mirror = (row + lane == NB - 1).astype(BF)
        same = (row < 64) == (lane >= 64)
        for head in range(HEADS):
            half = (head % 2) * PAGE
            block = slide_acc[head // 2, :, half : half + PAGE]
            high = block.astype(BF)
            low = (block - high.astype(F32)).astype(BF)
            block = dot(mirror, high) + dot(mirror, low)
            block = jnp.concatenate([block, jnp.zeros_like(block)], axis=1)
            slid = pltpu.roll(block, 0, 1, stride=1, stride_axis=0)
            slide_sum_ref[head : head + 1, :] = jnp.sum(slid, axis=0, keepdims=True)
            block = jnp.where(same, box_acc[:, head * NB : (head + 1) * NB], 0.0)
            slid = pltpu.roll(block, 0, 1, stride=1, stride_axis=0)
            box_sum_ref[1, head : head + 1, :] = jnp.sum(slid[:64], axis=0, keepdims=True)
            box_sum_ref[0, head : head + 1, :] = jnp.sum(slid[64:], axis=0, keepdims=True)


def attend_back(queries, keys, values, d_context, boxes, flipped, prob):
    width = HEADS * HEAD_DIM
    wide = pl.BlockSpec((PAGE, width), lambda i: (i, 0))
    return pl.pallas_call(
        attend_back_kernel,
        grid=(PAGES,),
        in_specs=[
            wide,
            wide,
            wide,
            wide,
            pl.BlockSpec((PAGE, NB), lambda i: (i, 0)),
            pl.BlockSpec((NB, PAGE), lambda i: (0, i)),
            pl.BlockSpec((1, PAIRS, PAGE, 2 * PAGE), lambda i: (i, 0, 0, 0)),
        ],
        out_specs=(
            pl.BlockSpec((PAGE, 3 * width), lambda i: (i, 0)),
            pl.BlockSpec((HEADS, 2 * PAGE), lambda i: (0, 0)),
            pl.BlockSpec((2, HEADS, NB), lambda i: (0, 0, 0)),
            pl.BlockSpec((8, 3 * width), lambda i: (0, 0)),
        ),
        out_shape=(
            jax.ShapeDtypeStruct((PAGES * PAGE, 3 * width), BF),
            jax.ShapeDtypeStruct((HEADS, 2 * PAGE), F32),
            jax.ShapeDtypeStruct((2, HEADS, NB), F32),
            jax.ShapeDtypeStruct((8, 3 * width), F32),
        ),
        scratch_shapes=[
            pltpu.VMEM((PAIRS, PAGE, 2 * PAGE), F32),
            pltpu.VMEM((NB, HEADS * NB), F32),
            pltpu.VMEM((PAIRS, PAGE, 2 * PAGE), F32),
            pltpu.VMEM((PAIRS, PAGE, 2 * PAGE), BF),
            pltpu.VMEM((PAGE, HEADS * NB), BF),
        ],
        compiler_params=pltpu.CompilerParams(vmem_limit_bytes=VMEM_LIMIT),
        cost_estimate=cost(14),
    )(queries, keys, values, d_context, boxes, flipped, prob)


ROWS_AT_ONCE = 32
Q_BIAS, V_BIAS, O_BIAS, GAIN1, SHIFT1, I_BIAS, U_BIAS, GAIN2, SHIFT2 = range(9)
SPOTS = (0, 1, 2, 3, 4, 5, 9, 10, 11)
TABLE_SPOT = 12


def fetch(blocks, held, sem):
    copies = [
        pltpu.make_async_copy(blocks[k], held.at[k], sem.at[k]) for k in range(len(blocks))
    ]
    for copy in copies:
        copy.start()
    return copies


def norm_parts(values):
    center = jnp.mean(values, axis=-1, keepdims=True)
    centered = values - center
    spread = lax.rsqrt(jnp.mean(centered * centered, axis=-1, keepdims=True) + EPSILON)
    return centered * spread, spread


def norm_back(normed, spread, pulled):
    level = jnp.mean(pulled, axis=-1, keepdims=True)
    slope = jnp.mean(pulled * normed, axis=-1, keepdims=True)
    return spread * (pulled - level - normed * slope)


def fold_rows(values):
    return jnp.sum(values.reshape(-1, 8, values.shape[-1]), axis=0)


def run(length, kernel, shapes, order, ins, blocks, scratch, far=()):
    near_spec = pl.BlockSpec(memory_space=pltpu.VMEM)
    far_spec = pl.BlockSpec(memory_space=pltpu.HBM)
    return pl.pallas_call(
        kernel,
        out_shape=tuple(jax.ShapeDtypeStruct(item[0], item[1]) for item in shapes),
        in_specs=[pl.BlockSpec(memory_space=pltpu.SMEM)]
        + [near_spec] * len(ins)
        + [far_spec] * (len(far) + len(blocks)),
        out_specs=tuple(far_spec if len(item) > 2 else near_spec for item in shapes),
        scratch_shapes=scratch,
        compiler_params=pltpu.CompilerParams(vmem_limit_bytes=VMEM_LIMIT),
        cost_estimate=cost(length),
    )(order, *ins, *far, *blocks)


def begin(source, target, sem):
    copy = pltpu.make_async_copy(source, target, sem)
    copy.start()
    return copy


def finish(copies):
    for copy in copies:
        copy.wait()


def each_rows(group, body, carry):
    def step(c, carry):
        return body(pl.ds(pl.multiple_of(c * ROWS_AT_ONCE, ROWS_AT_ONCE), ROWS_AT_ONCE), carry)

    return lax.fori_loop(group[0], group[-1] + 1, step, carry)


def row_groups(count):
    chunks = count // ROWS_AT_ONCE
    edges = sorted({chunks * i // 4 for i in range(5)})
    return [range(low, high) for low, high in zip(edges, edges[1:])]


def project_kernel(order_ref, x_ref, *refs):
    blocks = refs[:8]
    q_ref, k_ref, v_ref, vector_ref, table_ref, held, sem = refs[8:]
    copies = fetch(blocks, held, sem)
    x = jnp.concatenate([x_ref[:, lanes(order_ref, k, 128)] for k in range(8)], axis=1)
    for copy in copies:
        copy.wait()
    rows = (held.shape[1] - 16) // 3

    def piece(k, spot):
        return held[k, pl.ds(3 * rows, 16), pl.ds(spot % 8 * 128, 128)].astype(F32)[
            spot // 8 : spot // 8 + 1
        ]

    for k in range(8):
        for i, spot in enumerate(SPOTS):
            if i == I_BIAS:
                for part in range(4):
                    at = pl.multiple_of(order_ref[k] * 512 + part * 128, 128)
                    vector_ref[i : i + 1, pl.ds(at, 128)] = piece(k, spot + part)
            else:
                vector_ref[i : i + 1, lanes(order_ref, k, 128)] = piece(k, spot)
        for part in range(6):
            table_ref[order_ref[k] * 6 + part] = piece(k, TABLE_SPOT + part)
    half = q_ref.shape[1] // 2

    @pl.loop(0, 2)
    def _(part):
        at = pl.ds(pl.multiple_of(part * half, half), half)
        for j, out_ref in ((1, k_ref), (0, q_ref), (2, v_ref)):
            weight = jnp.concatenate(
                [held[k, j * rows : (j + 1) * rows, at] for k in range(8)], axis=0
            )
            found = dot(x, weight)
            if j == 0:
                found = (found + vector_ref[Q_BIAS : Q_BIAS + 1, at]) * HEAD_DIM ** (-0.5)
            if j == 2:
                found = found + vector_ref[V_BIAS : V_BIAS + 1, at]
            out_ref[:, at] = found.astype(BF)


def project(order, x, blocks):
    count, width = x.shape
    return run(
        12,
        project_kernel,
        [((count, width), BF)] * 3 + [((16, 4 * width), F32), ((48, 1, 128), F32)],
        order,
        [x],
        blocks,
        [pltpu.VMEM((8,) + blocks[0].shape, BF), pltpu.SemaphoreType.DMA((8,))],
    )


def output_kernel(order_ref, c_ref, spread_ref, hidden_ref, vector_ref, *refs):
    blocks = refs[:8]
    context_ref, normed_ref, deviation_ref, low_ref, held, sem = refs[8:]
    copies = fetch(blocks, held, sem)
    context_ref[...] = dot(spread_ref[...], c_ref[...]).astype(BF)
    x = jnp.concatenate([context_ref[:, lanes(order_ref, k, 128)] for k in range(8)], axis=1)
    for copy in copies:
        copy.wait()
    width = hidden_ref.shape[1]
    normed_ref[...] = dot(x, held[...].reshape(-1, width))
    bias = vector_ref[O_BIAS : O_BIAS + 1, :width]
    gain = vector_ref[GAIN1 : GAIN1 + 1, :width]
    offset = vector_ref[SHIFT1 : SHIFT1 + 1, :width]

    def body(at, carry):
        normed, deviation = norm_parts(
            hidden_ref[at, :].astype(F32) + (normed_ref[at, :] + bias)
        )
        normed_ref[at, :] = normed
        deviation_ref[at, :] = deviation
        low_ref[at, :] = (normed * gain + offset).astype(BF)
        return carry

    each_rows(range(hidden_ref.shape[0] // ROWS_AT_ONCE), body, 0)


def output_block(order, context, spread, hidden, vectors, blocks):
    count, width = hidden.shape
    return run(
        7,
        output_kernel,
        [((count, width), BF), ((count, width), F32), ((count, 1), F32), ((count, width), BF)],
        order,
        [context, spread, hidden, vectors],
        blocks,
        [pltpu.VMEM((8,) + blocks[0].shape, BF), pltpu.SemaphoreType.DMA((8,))],
    )


def inner_kernel(tiles, order_ref, x_ref, vector_ref, *refs):
    blocks = refs[:8]
    active_out, steep_out, held, first, second, active_ref, steep_ref, sem, out_sem = refs[8:]
    rows = blocks[0].shape[0]
    size = active_out.shape[1] // tiles
    for t in range(tiles):
        at = slice(t * size, (t + 1) * size)
        for k in range(8):
            begin(blocks[k].at[:, at], held.at[t, pl.ds(k * rows, rows), :], sem.at[t])
    x = jnp.concatenate([x_ref[:, lanes(order_ref, k, 128)] for k in range(8)], axis=1)

    def place(t):
        return pl.ds(pl.multiple_of(t * size, size), size)

    def multiply(t, target):
        for k in range(8):
            pltpu.make_async_copy(
                blocks[k].at[:, :size], held.at[t, pl.ds(k * rows, rows), :], sem.at[t]
            ).wait()
        target[...] = dot(x, held[t])

    def bend(t, source):
        bias = vector_ref[I_BIAS : I_BIAS + 1, place(t)]
        for c in range(x_ref.shape[0] // ROWS_AT_ONCE):
            row = slice(c * ROWS_AT_ONCE, (c + 1) * ROWS_AT_ONCE)
            inner = source[row] + bias
            share = 0.5 + 0.5 * lax.erf(inner * 0.5**0.5)
            active_ref[row, place(t)] = (inner * share).astype(BF)
            steep_ref[row, place(t)] = (
                share + inner * jnp.exp(-0.5 * inner * inner) * (2 * np.pi) ** -0.5
            ).astype(BF)

    def leave(t):
        at = place(t)
        return (
            pltpu.make_async_copy(active_ref.at[:, at], active_out.at[:, at], out_sem.at[0, t]),
            pltpu.make_async_copy(steep_ref.at[:, at], steep_out.at[:, at], out_sem.at[1, t]),
        )

    second[...] = jnp.zeros_like(second)

    @pl.loop(0, tiles // 2)
    def _(half):
        t = 2 * half
        before = jnp.maximum(t - 1, 0)
        multiply(t, first)
        bend(before, second)
        multiply(t + 1, second)
        bend(t, first)

        @pl.when(half > 0)
        def _():
            for copy in leave(before):
                copy.start()

        for copy in leave(t):
            copy.start()

    bend(tiles - 1, second)
    for copy in leave(tiles - 1):
        copy.start()
    for t in range(tiles):
        finish(leave(t))


def inner_block(order, x, vectors, blocks, tiles=8):
    count, width = x.shape
    wide = blocks[0].shape[1]
    return run(
        14,
        partial(inner_kernel, tiles),
        [((count, wide), BF, 1), ((count, wide), BF, 1)],
        order,
        [x, vectors],
        blocks,
        [
            pltpu.VMEM((tiles, width, wide // tiles), BF),
            pltpu.VMEM((count, wide // tiles), F32),
            pltpu.VMEM((count, wide // tiles), F32),
            pltpu.VMEM((count, wide), BF),
            pltpu.VMEM((count, wide), BF),
            pltpu.SemaphoreType.DMA((tiles,)),
            pltpu.SemaphoreType.DMA((2, tiles)),
        ],
    )


def outer_kernel(order_ref, vector_ref, a_far, normed_far, upstream_far, *refs):
    blocks = refs[:8]
    (
        out_far,
        second_far,
        d_outer_far,
        sum_ref,
        held,
        a_ref,
        normed_ref,
        upstream_ref,
        out_ref,
        second_ref,
        d_outer_ref,
        sem,
        in_sem,
        out_sem,
    ) = refs[8:]
    width = out_ref.shape[1]
    rows = blocks[0].shape[0]
    weights, lefts = [], []
    for k in range(8):
        at = lanes(order_ref, k, rows)
        lefts.append(begin(a_far.at[:, at], a_ref.at[k], in_sem.at[k]))
        weights.append(begin(blocks[k], held.at[k], sem.at[k]))
    late = [
        begin(normed_far, normed_ref, in_sem.at[8]),
        begin(upstream_far, upstream_ref, in_sem.at[9]),
    ]
    finish([lefts[0], weights[0]])
    second_ref[...] = dot(a_ref[0], held[0])

    @pl.loop(1, 8)
    def _(k):
        pltpu.make_async_copy(
            a_far.at[:, lanes(order_ref, k, rows)], a_ref.at[k], in_sem.at[k]
        ).wait()
        pltpu.make_async_copy(blocks[1], held.at[k], sem.at[k]).wait()
        second_ref[...] += dot(a_ref[k], held[k])

    finish(late)
    gain1 = vector_ref[GAIN1 : GAIN1 + 1, :width]
    shift1 = vector_ref[SHIFT1 : SHIFT1 + 1, :width]
    gain2 = vector_ref[GAIN2 : GAIN2 + 1, :width]
    shift2 = vector_ref[SHIFT2 : SHIFT2 + 1, :width]
    bias = vector_ref[U_BIAS : U_BIAS + 1, :width]
    sums = (jnp.zeros((8, width), F32),) * 3
    leaving = []
    for g, group in enumerate(row_groups(out_ref.shape[0])):

        def body(at, sums):
            first_out = normed_ref[at, :] * gain1 + shift1
            normed, deviation = norm_parts(first_out + (second_ref[at, :] + bias))
            out_ref[at, :] = (normed * gain2 + shift2).astype(BF)
            upstream = upstream_ref[at, :].astype(F32)
            d_second = norm_back(normed, deviation, upstream * gain2)
            second_ref[at, :] = d_second
            low = d_second.astype(BF)
            d_outer_ref[at, :] = low
            return (
                sums[0] + fold_rows(upstream * normed),
                sums[1] + fold_rows(upstream),
                sums[2] + fold_rows(low.astype(F32)),
            )

        sums = each_rows(group, body, sums)
        at = pl.ds(group[0] * ROWS_AT_ONCE, len(group) * ROWS_AT_ONCE)
        for i, (source, target) in enumerate(
            ((out_ref, out_far), (second_ref, second_far), (d_outer_ref, d_outer_far))
        ):
            leaving.append(begin(source.at[at], target.at[at], out_sem.at[i, g]))
    for i in range(3):
        sum_ref[i : i + 1, :] = jnp.sum(sums[i], axis=0, keepdims=True)
    finish(leaving)


def outer_block(order, active, normed, upstream, vectors, blocks):
    count, width = normed.shape
    return run(
        11.5,
        outer_kernel,
        [
            ((count, width), BF, 1),
            ((count, width), F32, 1),
            ((count, width), BF, 1),
            ((8, width), F32),
        ],
        order,
        [vectors],
        blocks,
        [
            pltpu.VMEM((8,) + blocks[0].shape, BF),
            pltpu.VMEM((8, count, active.shape[1] // 8), BF),
            pltpu.VMEM((count, width), F32),
            pltpu.VMEM((count, width), BF),
            pltpu.VMEM((count, width), BF),
            pltpu.VMEM((count, width), F32),
            pltpu.VMEM((count, width), BF),
            pltpu.SemaphoreType.DMA((8,)),
            pltpu.SemaphoreType.DMA((10,)),
            pltpu.SemaphoreType.DMA((3, 4)),
        ],
        [active, normed, upstream],
    )


def inner_back_kernel(order_ref, d_ref, steep_far, *refs):
    blocks = refs[:8]
    out_far, sum_ref, held, steep_ref, out_ref, sem, in_sem, out_sem = refs[8:]
    rows = blocks[0].shape[0]
    copies = []
    for k in range(8):
        at = lanes(order_ref, k, rows)
        copies.append(
            [
                begin(blocks[k], held.at[k], sem.at[k]),
                begin(steep_far.at[:, at], steep_ref.at[k], in_sem.at[k]),
            ]
        )

    @pl.loop(0, 8)
    def _(k):
        at = lanes(order_ref, k, rows)
        pltpu.make_async_copy(blocks[0], held.at[k], sem.at[k]).wait()
        pltpu.make_async_copy(steep_far.at[:, at], steep_ref.at[k], in_sem.at[k]).wait()
        low = (dot(d_ref[...], held[k], NT) * steep_ref[k].astype(F32)).astype(BF)
        out_ref[k] = low
        sum_ref[:, at] = fold_rows(low.astype(F32))
        begin(out_ref.at[k], out_far.at[:, at], out_sem.at[k])

    for k in range(8):
        pltpu.make_async_copy(
            out_ref.at[k], out_far.at[:, lanes(order_ref, k, rows)], out_sem.at[k]
        ).wait()


def inner_back(order, d_outer, steep, blocks):
    count, wide = steep.shape
    return run(
        10,
        inner_back_kernel,
        [((count, wide), BF, 1), ((8, wide), F32)],
        order,
        [d_outer],
        blocks,
        [
            pltpu.VMEM((8,) + blocks[0].shape, BF),
            pltpu.VMEM((8, count, wide // 8), BF),
            pltpu.VMEM((8, count, wide // 8), BF),
            pltpu.SemaphoreType.DMA((8,)),
            pltpu.SemaphoreType.DMA((8,)),
            pltpu.SemaphoreType.DMA((8,)),
        ],
        [steep],
    )


def first_back_kernel(
    order_ref, d_ref, deviation_ref, vector_ref, second_far, normed_far, *refs
):
    blocks = refs[:8]
    (
        summed_far,
        low_far,
        sum_ref,
        held,
        second_ref,
        normed_ref,
        summed_ref,
        low_ref,
        sem,
        in_sem,
        out_sem,
    ) = refs[8:]
    copies = fetch(blocks, held, sem)
    late = [
        begin(second_far, second_ref, in_sem.at[0]),
        begin(normed_far, normed_ref, in_sem.at[1]),
    ]
    width = summed_ref.shape[1]
    rows = blocks[0].shape[0]

    @pl.loop(0, 4)
    def _(pair):
        k = 2 * pair
        pltpu.make_async_copy(blocks[0], held.at[k], sem.at[k]).wait()
        pltpu.make_async_copy(blocks[0], held.at[k + 1], sem.at[k + 1]).wait()
        weight = jnp.concatenate([held[k], held[k + 1]], axis=0)
        part = dot(d_ref[...], weight, NT)
        summed_ref[:, lanes(order_ref, k, rows)] = part[:, :rows]
        summed_ref[:, lanes(order_ref, k + 1, rows)] = part[:, rows:]

    finish(late)
    gain = vector_ref[GAIN1 : GAIN1 + 1, :width]
    sums = (jnp.zeros((8, width), F32),) * 3
    leaving = []
    for g, group in enumerate(row_groups(summed_ref.shape[0])):

        def body(at, sums):
            d_first = second_ref[at, :] + summed_ref[at, :]
            normed = normed_ref[at, :]
            d_summed = norm_back(normed, deviation_ref[at, :], d_first * gain)
            summed_ref[at, :] = d_summed
            low = d_summed.astype(BF)
            low_ref[at, :] = low
            return (
                sums[0] + fold_rows(d_first * normed),
                sums[1] + fold_rows(d_first),
                sums[2] + fold_rows(low.astype(F32)),
            )

        sums = each_rows(group, body, sums)
        at = pl.ds(group[0] * ROWS_AT_ONCE, len(group) * ROWS_AT_ONCE)
        leaving.append(begin(summed_ref.at[at], summed_far.at[at], out_sem.at[0, g]))
        leaving.append(begin(low_ref.at[at], low_far.at[at], out_sem.at[1, g]))
    for i in range(3):
        sum_ref[i : i + 1, :] = jnp.sum(sums[i], axis=0, keepdims=True)
    finish(leaving)


def first_back(order, d_inner, d_second, normed, deviation, vectors, blocks):
    count, width = normed.shape
    return run(
        16,
        first_back_kernel,
        [((count, width), F32, 1), ((count, width), BF, 1), ((8, width), F32)],
        order,
        [d_inner, deviation, vectors],
        blocks,
        [
            pltpu.VMEM((8,) + blocks[0].shape, BF),
            pltpu.VMEM((count, width), F32),
            pltpu.VMEM((count, width), F32),
            pltpu.VMEM((count, width), F32),
            pltpu.VMEM((count, width), BF),
            pltpu.SemaphoreType.DMA((8,)),
            pltpu.SemaphoreType.DMA((2,)),
            pltpu.SemaphoreType.DMA((2, 4)),
        ],
        [d_second, normed],
    )


def context_back_kernel(order_ref, d_ref, spread_ref, *refs):
    blocks = refs[:8]
    out_ref, held, kept, sem = refs[8:]
    copies = fetch(blocks, held, sem)
    rows = blocks[0].shape[0]
    for copy in copies:
        copy.wait()

    @pl.loop(0, 4)
    def _(pair):
        k = 2 * pair
        weight = jnp.concatenate([held[k], held[k + 1]], axis=0)
        part = dot(d_ref[...], weight, NT).astype(BF)
        kept[:, lanes(order_ref, k, rows)] = part[:, :rows]
        kept[:, lanes(order_ref, k + 1, rows)] = part[:, rows:]

    out_ref[...] = dot(spread_ref[...], kept[...]).astype(BF)


def context_back(order, d_attn, spread, blocks):
    count, width = d_attn.shape
    return run(
        6.5,
        context_back_kernel,
        [((spread.shape[0], width), BF)],
        order,
        [d_attn, spread],
        blocks,
        [
            pltpu.VMEM((8,) + blocks[0].shape, BF),
            pltpu.VMEM((count, width), BF),
            pltpu.SemaphoreType.DMA((8,)),
        ],
    )[0]


def input_back_kernel(order_ref, d_ref, spread_ref, summed_far, *refs):
    blocks = refs[:8]
    out_far, held, kept, summed_ref, out_ref, sem, in_sem, out_sem = refs[8:]
    copies = fetch(blocks, held, sem)
    late = begin(summed_far, summed_ref, in_sem.at[0])
    rows = (blocks[0].shape[0] - 16) // 3
    width = summed_ref.shape[1]

    @pl.loop(0, 3)
    def _(j):
        at = pl.ds(pl.multiple_of(j * width, width), width)
        kept[:, at] = dot(spread_ref[...], d_ref[:, at]).astype(BF)

    finish(copies)
    late.wait()

    @pl.loop(0, 4)
    def _(pair):
        k = 2 * pair
        weight = jnp.concatenate(
            [
                jnp.concatenate(
                    [held[k, j * rows : (j + 1) * rows], held[k + 1, j * rows : (j + 1) * rows]],
                    axis=0,
                )
                for j in range(3)
            ],
            axis=1,
        )
        part = dot(kept[...], weight, NT)
        for i in range(2):
            at = lanes(order_ref, k + i, rows)
            out_ref[k + i] = summed_ref[:, at] + part[:, i * rows : (i + 1) * rows]
            begin(out_ref.at[k + i], out_far.at[:, at], out_sem.at[k + i])

    for k in range(8):
        at = lanes(order_ref, k, rows)
        pltpu.make_async_copy(out_ref.at[k], out_far.at[:, at], out_sem.at[k]).wait()


def input_back(order, d_mixed, spread, d_summed, blocks):
    count, width = d_summed.shape
    return run(
        12.5,
        input_back_kernel,
        [((count, width), F32, 1)],
        order,
        [d_mixed, spread],
        blocks,
        [
            pltpu.VMEM((8,) + blocks[0].shape, BF),
            pltpu.VMEM((count, 3 * width), BF),
            pltpu.VMEM((count, width), F32),
            pltpu.VMEM((8, count, width // 8), F32),
            pltpu.SemaphoreType.DMA((8,)),
            pltpu.SemaphoreType.DMA((1,)),
            pltpu.SemaphoreType.DMA((8,)),
        ],
        [d_summed],
    )[0]


def small_kernel(
    order_ref,
    slide_ref,
    box_ref,
    bias_ref,
    first_ref,
    inner_ref,
    second_ref,
    *refs,
):
    outs, flat = refs[:8], refs[8]
    spot = one_hot(
        (2 * PAGE, NB),
        lambda c, bucket: (jnp.clip(PAGE - 1 - c, -64, 63) + 64 == bucket) & (c < 2 * PAGE - 1),
    ).astype(F32)
    by_head = [precise(slide_ref[...], spot)]
    by_head += [pltpu.roll(box_ref[i], 65, 1) for i in range(2)]
    heads = one_hot((NB, HEADS), lambda r, c: r % 16 == c).astype(F32)
    mine = one_hot((NB, NB), lambda r, c: r // 16 == c % 8)
    rows = one_hot((16, NB), lambda r, c: c // 8 == r).astype(F32)
    for kind in range(3):
        spread = jnp.where(mine, precise(heads, by_head[kind]), 0.0)
        found = precise(rows, spread, NT)
        for i in range(16):
            flat[16 * kind + i] = found[i : i + 1]
    width = first_ref.shape[1]
    bias = jnp.sum(bias_ref[...], axis=0, keepdims=True)
    inner = jnp.sum(inner_ref[...], axis=0, keepdims=True)
    bias_ref[0:1, :] = bias
    inner_ref[0:1, :] = inner
    for k in range(8):
        out_ref = outs[k]
        at = lanes(order_ref, k, 128)
        out_ref[0:1, :] = bias_ref[0:1, at]
        out_ref[1:2, :] = bias_ref[
            0:1, pl.ds(pl.multiple_of(2 * width + order_ref[k] * 128, 128), 128)
        ]
        out_ref[2:3, :] = first_ref[2:3, at]
        out_ref[3:5, :] = first_ref[0:2, at]
        for part in range(4):
            piece = pl.ds(pl.multiple_of(order_ref[k] * 512 + part * 128, 128), 128)
            out_ref[5 + part : 6 + part, :] = inner_ref[0:1, piece]
        out_ref[9:10, :] = second_ref[2:3, at]
        out_ref[10:12, :] = second_ref[0:2, at]
        for part in range(6):
            out_ref[12 + part : 13 + part, :] = flat[order_ref[k] * 6 + part]
        out_ref[18:, :] = jnp.zeros((6, 128), F32)


def small_blocks(order, sums):
    return pl.pallas_call(
        small_kernel,
        out_shape=(jax.ShapeDtypeStruct((24, 128), F32),) * 8,
        in_specs=[pl.BlockSpec(memory_space=pltpu.SMEM)]
        + [pl.BlockSpec(memory_space=pltpu.VMEM)] * 6,
        out_specs=(pl.BlockSpec(memory_space=pltpu.VMEM),) * 8,
        scratch_shapes=[pltpu.VMEM((48, 1, 128), F32)],
        compiler_params=pltpu.CompilerParams(vmem_limit_bytes=VMEM_LIMIT),
        cost_estimate=cost(3),
    )(order, *sums)


def on_device(line, mesh_size, *args):
    (
        hidden_in,
        cotangent,
        segment_ids,
        box_left,
        box_top,
        query_weight,
        query_bias,
        key_weight,
        value_weight,
        value_bias,
        output_weight,
        output_bias,
        first_gain,
        first_shift,
        inner_weight,
        inner_bias,
        outer_weight,
        outer_bias,
        second_gain,
        second_shift,
        bucket_table,
    ) = args
    slot_count = segment_ids.shape[1]
    width = hidden_in.shape[1]
    vectors = (
        query_bias,
        value_bias,
        output_bias,
        first_gain,
        first_shift,
        inner_bias,
        outer_bias,
        second_gain,
        second_shift,
        bucket_table,
    )
    phase = lax.optimization_barrier
    if line:
        order = block_order(lax.axis_index("fsdp"))
        packed = pack((query_weight, key_weight, value_weight), vectors)
        in_blocks = [packed, hop(packed, NEAR), hop(packed, FAR)]
    else:
        order = jnp.arange(8, dtype=jnp.int32)

        def whole(shard):
            return lax.all_gather(shard, "fsdp", axis=0, tiled=True)

        def blocks_of(shard):
            full = whole(shard)
            return list(full.reshape(8, full.shape[0] // 8, full.shape[1]))

        small = jnp.concatenate([whole(item).reshape(8, -1) for item in vectors], axis=1)
        small = jnp.pad(small, ((0, 0), (0, 16 * width - small.shape[1])))
        in_blocks = jnp.concatenate(
            [whole(item).reshape(8, -1, width) for item in (query_weight, key_weight, value_weight)]
            + [small.reshape(8, 16, width)],
            axis=1,
        )
        in_blocks = list(in_blocks)
        output_blocks = blocks_of(output_weight)
        inner_blocks = blocks_of(inner_weight)
        outer_blocks = blocks_of(outer_weight)

    slot = lax.iota(jnp.int32, slot_count)
    pages = lax.iota(jnp.int32, PAGES)
    segments = segment_ids[0]
    member = segments[None, :] == pages[:, None]
    lengths = jnp.sum(member, axis=1, dtype=jnp.int32)
    starts = jnp.sum(segments[None, :] < pages[:, None], axis=1, dtype=jnp.int32)
    start_of = jnp.sum(jnp.where(member, starts[:, None], 0), axis=0)
    target = segments * PAGE + slot - start_of
    padded = lax.iota(jnp.int32, PAGES * PAGE)
    spread = (padded[:, None] == target[None, :]).astype(BF)
    gather = (padded[None, :] == target[:, None]).astype(BF)
    coords = lax.iota(jnp.int32, NB) % 64
    sides = jnp.where(padded[None, :NB] < 64, box_left[0][:, None], box_top[0][:, None])
    boxes = dot(spread, (sides == coords[None, :]).astype(BF)).astype(BF)
    turned = jnp.where(padded[:NB, None] < 64, box_top[0][None, :], box_left[0][None, :])
    turned = (turned == 63 - coords[:, None]).astype(BF)
    flipped = dot(turned, spread, NT).astype(BF)
    hidden = dot(spread, hidden_in).astype(BF)

    if line:
        in_blocks, hidden, boxes, flipped, gather, spread, inner_weight = phase(
            (in_blocks, hidden, boxes, flipped, gather, spread, inner_weight)
        )
        own, near, far = in_blocks
        both = hop(near, FAR)
        twins = [hop(item, TWIN) for item in (own, near, far)]
        inner_near = hop(inner_weight, NEAR)
        both, twins, inner_near, inner_weight, output_weight = phase(
            (both, twins, inner_near, inner_weight, output_weight)
        )
        in_blocks = [own, near, far, both] + twins + [hop(both, TWIN)]
        inner_far = hop(inner_weight, FAR)
        output_near, output_far = hop(output_weight, NEAR), hop(output_weight, FAR)
    queries, keys, values, vector, table = project(order, hidden, in_blocks)
    lookup, slide = make_tables(table)
    if line:
        (
            queries,
            keys,
            values,
            lookup,
            slide,
            inner_near,
            inner_far,
            output_near,
            output_far,
            outer_weight,
        ) = phase(
            (
                queries,
                keys,
                values,
                lookup,
                slide,
                inner_near,
                inner_far,
                output_near,
                output_far,
                outer_weight,
            )
        )
        outer_near = hop(outer_weight, NEAR)
        output_blocks = [output_weight, output_near, output_far, hop(output_near, FAR)]
    context, prob = attend(lengths, queries, keys, values, boxes, lookup, slide)
    if line:
        context, outer_near, output_blocks, inner_near, inner_far = phase(
            (context, outer_near, output_blocks, inner_near, inner_far)
        )
        inner_blocks = [inner_weight, inner_near, inner_far, hop(inner_near, FAR)]
        outer_far = hop(outer_weight, FAR)
        output_blocks = output_blocks + [hop(item, TWIN) for item in output_blocks]
        inner_twins = [hop(item, TWIN) for item in inner_blocks[:3]]
    context, normed, deviation, first_low = output_block(
        order, context, gather, hidden_in, vector, output_blocks
    )
    if line:
        first_low, inner_blocks, inner_twins, outer_near, outer_far = phase(
            (first_low, inner_blocks, inner_twins, outer_near, outer_far)
        )
        outer_blocks = [outer_weight, outer_near, outer_far, hop(outer_near, FAR)]
        inner_blocks = inner_blocks + inner_twins + [hop(inner_blocks[3], TWIN)]
        outer_twins = [hop(item, TWIN) for item in outer_blocks[:3]]
    active, steep = inner_block(order, first_low, vector, inner_blocks)
    if line:
        active, outer_blocks, outer_twins = phase((active, outer_blocks, outer_twins))
        outer_blocks = outer_blocks + outer_twins + [hop(outer_blocks[3], TWIN)]
    layer_out, d_second, d_outer, second_sums = outer_block(
        order, active, normed, cotangent, vector, outer_blocks
    )

    if line:
        send = turned_blocks(order, 4, active, d_outer)
        d_outer, send = phase((d_outer, send))
        other2 = to_twin(send)
    d_inner, inner_sums = inner_back(order, d_outer, steep, outer_blocks)
    if line:
        d_inner, other2 = phase((d_inner, other2))
        stay2, away2 = turned_blocks(order, 0, active, d_outer, other2)
        d_inner, stay2, away2 = phase((d_inner, stay2, away2))
        other2 = hop(away2, FAR)
        d_inner, stay2 = phase((d_inner, stay2))
    d_summed, d_attn, first_sums = first_back(
        order, d_inner, d_second, normed, deviation, vector, inner_blocks
    )
    if line:
        pairs1 = ((first_low, d_inner), (context, d_attn))
        send = grad_blocks(order, 4, pairs1, 1024)
        d_attn, send, stay2, other2 = phase((d_attn, send, stay2, other2))
        other1 = to_twin(send)
        stay2, away2 = fold_far(stay2, other2)
        other2 = hop(away2, NEAR)
    d_context = context_back(order, d_attn, spread, output_blocks)
    if line:
        d_context, other1, stay2 = phase((d_context, other1, stay2))
        stay1, away1 = grad_blocks(order, 0, pairs1, 1024, other1)
        d_context, stay1, away1, stay2, other2 = phase(
            (d_context, stay1, away1, stay2, other2)
        )
        other1 = hop(away1, FAR)
        kept2, sent2 = cut(stay2 + other2, 1)
        other2 = trade(sent2, 1)
    d_mixed, slide_sum, box_sum, bias_sum = attend_back(
        queries, keys, values, d_context, boxes, flipped, prob
    )
    sums = (slide_sum, box_sum, bias_sum, first_sums, inner_sums, second_sums)
    if line:
        pairs = ((hidden, d_mixed),)
        d_mixed, kept2, other2, stay1, sums = phase((d_mixed, kept2, other2, stay1, sums))
        kept2, sent2 = cut(kept2 + other2, 2)
        other2 = trade(sent2, 2)
        send = grad_blocks(order, 4, pairs, 1024)
        d_mixed, send, kept2, other2, stay1, other1, sums = phase(
            (d_mixed, send, kept2, other2, stay1, other1, sums)
        )
        other = to_twin(send)
        stay1, away1 = fold_far(stay1, other1)
        other1 = hop(away1, NEAR)
        kept2 = kept2 + other2
        other2 = trade(kept2, 2)
    small = small_blocks(order, sums)
    if line:
        d_mixed, other, small, stay1, kept2 = phase((d_mixed, other, small, stay1, kept2))
        stay, away = grad_blocks(order, 0, pairs, 1024, other)
        d_mixed, stay, away, stay1, other1, kept2, other2, small = phase(
            (d_mixed, stay, away, stay1, other1, kept2, other2, small)
        )
        other = hop(away, FAR)
        small_other = to_twin(small[4:])
        kept1, sent1 = cut(stay1 + other1, 1)
        other1 = trade(sent1, 1)
    input_grad = input_back(order, d_mixed, gather, d_summed, in_blocks)
    if line:
        stay, other, input_grad, small, small_other, kept1, other1, kept2, other2 = phase(
            (stay, other, input_grad, small, small_other, kept1, other1, kept2, other2)
        )
        stay, away = fold_far(stay, other)
        other = hop(away, NEAR)
        kept1, sent1 = cut(kept1 + other1, 2)
        other1 = trade(sent1, 2)
        kept2 = paste(kept2, other2, 2)
        other2 = trade(kept2, 1)
        small = [small[i] + small_other[i] for i in range(4)]
        small_other = hop(jnp.stack(small[2:]), FAR)
        stay, other, small, small_other, kept1, other1, kept2, other2 = phase(
            (stay, other, small, small_other, kept1, other1, kept2, other2)
        )
        kept, sent = cut(stay + other, 1)
        other = trade(sent, 1)
        kept1 = kept1 + other1
        other1 = trade(kept1, 2)
        small = small[0] + small_other[0], small[1] + small_other[1]
        small_other = hop(small[1], NEAR)
        kept, other, kept1, other1, small, small_other, kept2, other2 = phase(
            (kept, other, kept1, other1, small, small_other, kept2, other2)
        )
        kept, sent = cut(kept + other, 2)
        other = trade(sent, 2)
        kept1 = paste(kept1, other1, 2)
        other1 = trade(kept1, 1)
        small = small[0] + small_other
        small_other = trade(small, 1)
        outer_own = paste(kept2, other2, 1).T.astype(F32)
        kept, other, kept1, other1, small, small_other, outer_own = phase(
            (kept, other, kept1, other1, small, small_other, outer_own)
        )
        kept = kept + other
        other = trade(kept, 2)
        small = small + small_other
        small_other = trade(small, 2)
        inner_own = paste(kept1, other1, 1).astype(F32)
        kept, other, small, small_other, inner_own = phase(
            (kept, other, small, small_other, inner_own)
        )
        kept = paste(kept, other, 2)
        other = trade(kept, 1)
        small = (small + small_other).reshape(-1)
        kept, other, small = phase((kept, other, small))
        in_own = paste(kept, other, 1)
        inner_own, output_own = inner_own[:, : 4 * width], inner_own[:, 4 * width :]
        cuts = np.cumsum([0] + [item.shape[0] for item in vectors])
        owned = [small[cuts[i] : cuts[i + 1]] for i in range(len(vectors))]
    else:

        def reduce(value):
            value = lax.psum_scatter(value, "fsdp", scatter_dimension=0, tiled=True)
            return lax.psum(value, "dp")

        small = jnp.stack(small)[:, :18].reshape(8, -1)
        edges = np.cumsum([0] + [item.shape[0] * mesh_size // 8 for item in vectors])
        owned = [
            reduce(small[:, edges[i] : edges[i + 1]].reshape(-1)) for i in range(len(vectors))
        ]
        outer_own = reduce(dot(active, d_outer, TN).astype(BF))
        inner_own = reduce(dot(first_low, d_inner, TN).astype(BF))
        output_own = reduce(dot(context, d_attn, TN).astype(BF))
        in_own = reduce(dot(hidden, d_mixed, TN).astype(BF))
    in_own = in_own.astype(F32)
    return (
        layer_out,
        input_grad,
        in_own[:, :width],
        owned[0],
        in_own[:, width : 2 * width],
        in_own[:, 2 * width :],
        owned[1],
        output_own.astype(F32),
        owned[2],
        owned[3],
        owned[4],
        inner_own.astype(F32),
        owned[5],
        outer_own.astype(F32),
        owned[6],
        owned[7],
        owned[8],
        owned[9],
    )


def solution(mesh):
    line = mesh.shape["fsdp"] == 8 and mesh.shape["dp"] == 4
    both, across, flat = P(("fsdp", "dp"), None), P("fsdp", None), P("fsdp")
    return jax.shard_map(
        partial(on_device, line, mesh.shape["fsdp"]),
        mesh=mesh,
        in_specs=(both,) * 5
        + (across, flat, across, across, flat, across, flat, flat, flat)
        + (across, flat, across, flat, flat, flat, flat),
        out_specs=(both, both)
        + (across, flat, across, across, flat, across, flat, flat, flat)
        + (across, flat, across, flat, flat, flat, flat),
        check_vma=False,
    )
```

profile of v0, /device:TPU:0, one launch (start us, length us, event | category | flops | bytes accessed | tf_op | source)
XLA Modules:
  0.0 393.9 jit_solution(1191609414592204381)
XLA Ops:
  17.7 7.7 %collective-permute-done.refs_1_ = bf16[400,1024]{1,0:T(8,128)(2,1)S(1)} collective-permute-done((bf16[400,1024]{1,0:T(8,128)(2,1)}, bf16[400,1024]{1,0:T(8,128)(2,1)S(1)}, u32[]{:S(2)}, u32[]{:S(2)}) %collective-permute-start) | collective-permute-done | bytes 819232 | tf_op jit(solution)/shard_map/ppermute | solution.py:56
  29.1 19.5 %collective-permute-done.2.refs_3_ = bf16[400,1024]{1,0:T(8,128)(2,1)} collective-permute-done((bf16[400,1024]{1,0:T(8,128)(2,1)S(1)}, bf16[400,1024]{1,0:T(8,128)(2,1)}, u32[]{:S(2)}, u32[]{:S(2)}) %collective-permute-start.2) | collective-permute-done | bytes 819232 | tf_op jit(solution)/shard_map/ppermute | solution.py:56
  54.6 13.0 %shard_map.359 = (bf16[1024,1024]{1,0:T(8,128)(2,1)}, bf16[1024,1024]{1,0:T(8,128)(2,1)}, bf16[1024,1024]{1,0:T(8,128)(2,1)}, f32[16,4096]{1,0:T(8,128)}, f32[48,1,128]{2,1,0:T(1,128)}) custom-call(s32[8]{0:T(128)} %fusion.19.order_ref, bf16[1024,1024]{1,0:T(8,128)(2,1)} %fusion.5.x_ref.refs_0_, bf16[400,1024]{1,0:T(8,128)(2,1)} %shard_map.358.refs_0_, ...), custom_call_target="tpu_custom_call" | custom-call | flops 3600000000 | bytes 1 | tf_op jit(solution)/shard_map/pallas_call | solution.py:524
  73.3 14.6 %shard_map.361 = (bf16[1024,1024]{1,0:T(8,128)(2,1)}, bf16[8,8,128,256]{3,2,1,0:T(8,128)(2,1)}) custom-call(s32[8]{0:T(128)} %get-tuple-element.536.length_ref, bf16[1024,1024]{1,0:T(8,128)(2,1)} %get-tuple-element.278.q_ref, bf16[1024,1024]{1,0:T(8,128)(2,1)} %get-tuple-element.279.k_ref, bf16[1024,1024]{1,0:T(8,128)(2,1)} %get-tuple-element.280.v_ref, ...), custom_call_target="tpu_custom_call" | custom-call | flops 4050000128 | bytes 1 | tf_op jit(solution)/shard_map/pallas_call | solution.py:342
  93.4 12.0 %shard_map.362 = (bf16[544,1024]{1,0:T(8,128)(2,1)}, f32[544,1024]{1,0:T(8,128)}, f32[544,1]{1,0:T(8,128)}, bf16[544,1024]{1,0:T(8,128)(2,1)}) custom-call(s32[8]{0:T(128)} %fusion.19.order_ref, bf16[1024,1024]{1,0:T(8,128)(2,1)} %get-tuple-element.290.c_ref, bf16[544,1024]{1,0:T(8,128)(2,1)} %fusion.4.spread_ref, bf16[544,1024]{1,0:T(8,128)(2,1)} %hidden_ref.1, ...), custom_call_target="tpu_custom_call" | custom-call | flops 2100000000 | bytes 1 | tf_op jit(solution)/shard_map/pallas_call | solution.py:524
  105.4 11.2 %collective-permute-done.17.refs_3_ = bf16[128,4096]{1,0:T(8,128)(2,1)} collective-permute-done((bf16[128,4096]{1,0:T(8,128)(2,1)}, bf16[128,4096]{1,0:T(8,128)(2,1)}, u32[]{:S(2)}, u32[]{:S(2)}) %collective-permute-start.17) | collective-permute-done | bytes 1048608 | tf_op jit(solution)/shard_map/ppermute | solution.py:56
  120.4 12.4 %shard_map.363 = (bf16[544,4096]{1,0:T(8,128)(2,1)}, bf16[544,4096]{1,0:T(8,128)(2,1)}) custom-call(s32[8]{0:T(128)} %fusion.19.order_ref, bf16[544,1024]{1,0:T(8,128)(2,1)} %get-tuple-element.300.x_ref.refs_0_, f32[16,4096]{1,0:T(8,128)} %get-tuple-element.268.vector_ref, bf16[128,4096]{1,0:T(8,128)(2,1)} %refs_0_.6, ...), custom_call_target="tpu_custom_call" | custom-call | flops 4200000000 | bytes 1 | tf_op jit(solution)/shard_map/pallas_call | solution.py:524
  136.7 15.7 %shard_map.364 = (bf16[544,1024]{1,0:T(8,128)(2,1)}, f32[544,1024]{1,0:T(8,128)}, bf16[544,1024]{1,0:T(8,128)(2,1)}, f32[8,1024]{1,0:T(8,128)}) custom-call(s32[8]{0:T(128)} %fusion.19.order_ref, f32[16,4096]{1,0:T(8,128)} %get-tuple-element.268.vector_ref, bf16[544,4096]{1,0:T(8,128)(2,1)} %get-tuple-element.311.a_far.left_ref, ...), custom_call_target="tpu_custom_call" | custom-call | flops 3449999872 | bytes 1 | tf_op jit(solution)/shard_map/pallas_call | solution.py:524
  152.4 9.1 %shard_map.365 = (bf16[1024,512]{1,0:T(8,128)(2,1)}, bf16[1024,512]{1,0:T(8,128)(2,1)}, bf16[1024,512]{1,0:T(8,128)(2,1)}, bf16[1024,512]{1,0:T(8,128)(2,1)}) custom-call(s32[8]{0:T(128)} %fusion.19.order_ref, bf16[544,4096]{1,0:T(8,128)(2,1)} %get-tuple-element.311.a_far.left_ref, bf16[544,1024]{1,0:T(8,128)(2,1)} %get-tuple-element.326.right_ref.d_ref), custom_call_target="tpu_custom_call" | custom-call | flops 2100000000 | bytes 1 | tf_op jit(solution)/shard_map/pallas_call | solution.py:152
  162.6 10.8 %shard_map.366 = (bf16[544,4096]{1,0:T(8,128)(2,1)}, f32[8,4096]{1,0:T(8,128)}) custom-call(s32[8]{0:T(128)} %fusion.19.order_ref, bf16[544,1024]{1,0:T(8,128)(2,1)} %get-tuple-element.326.right_ref.d_ref, bf16[544,4096]{1,0:T(8,128)(2,1)} %get-tuple-element.327.steep_far, bf16[512,1024]{1,0:T(8,128)(2,1)} %refs_0_.5, ...), custom_call_target="tpu_custom_call" | custom-call | flops 3000000000 | bytes 1 | tf_op jit(solution)/shard_map/pallas_call | solution.py:524
  174.4 10.5 %shard_map.367 = (bf16[2,1024,512]{2,1,0:T(8,128)(2,1)}, bf16[2,1024,512]{2,1,0:T(8,128)(2,1)}) custom-call(s32[8]{0:T(128)} %fusion.19.order_ref, bf16[544,4096]{1,0:T(8,128)(2,1)} %get-tuple-element.311.a_far.left_ref, bf16[544,1024]{1,0:T(8,128)(2,1)} %get-tuple-element.326.right_ref.d_ref, bf16[1024,512]{1,0:T(8,128)(2,1)} %copy-done.3, ...), custom_call_target="tpu_custom_call" | custom-call | flops 2100000000 | bytes 1 | tf_op jit(solution)/shard_map/pallas_call | solution.py:152
  185.6 13.7 %shard_map.368 = (f32[544,1024]{1,0:T(8,128)}, bf16[544,1024]{1,0:T(8,128)(2,1)}, f32[8,1024]{1,0:T(8,128)}) custom-call(s32[8]{0:T(128)} %fusion.19.order_ref, bf16[544,4096]{1,0:T(8,128)(2,1)} %get-tuple-element.342.d_ref.refs_2_, f32[544,1]{1,0:T(8,128)} %get-tuple-element.343.deviation_ref, f32[16,4096]{1,0:T(8,128)} %get-tuple-element.268.vector_ref, ...), custom_call_target="tpu_custom_call" | custom-call | flops 4800000000 | bytes 1 | tf_op jit(solution)/shard_map/pallas_call | solution.py:524
  199.3 10.3 %shard_map.369 = (bf16[128,5120]{1,0:T(8,128)(2,1)}, bf16[128,5120]{1,0:T(8,128)(2,1)}, bf16[128,5120]{1,0:T(8,128)(2,1)}, bf16[128,5120]{1,0:T(8,128)(2,1)}) custom-call(s32[8]{0:T(128)} %fusion.19.order_ref, bf16[544,1024]{1,0:T(8,128)(2,1)} %get-tuple-element.300.x_ref.refs_0_, bf16[544,1024]{1,0:T(8,128)(2,1)} %get-tuple-element.346.refs_1_, ...), custom_call_target="tpu_custom_call" | custom-call | flops 3000000000 | bytes 1 | tf_op jit(solution)/shard_map/pallas_call | solution.py:218
  216.4 8.5 %shard_map.370.g_ref = bf16[1024,1024]{1,0:T(8,128)(2,1)} custom-call(s32[8]{0:T(128)} %fusion.19.order_ref, bf16[544,1024]{1,0:T(8,128)(2,1)} %get-tuple-element.353.refs_3_.d_ref, bf16[1024,544]{1,0:T(8,128)(2,1)} %fusion.spread_ref, bf16[128,1024]{1,0:T(8,128)(2,1)} %refs_0_.7, bf16[128,1024]{1,0:T(8,128)(2,1)} %collective-permute-done.9.refs_1_, ...), custom_call_target="tpu_custom_call" | custom-call | flops 1950000000 | bytes 1 | tf_op jit(solution)/shard_map/pallas_call | solution.py:524
  224.9 11.4 %shard_map.371 = (bf16[2,128,5120]{2,1,0:T(8,128)(2,1)}, bf16[2,128,5120]{2,1,0:T(8,128)(2,1)}) custom-call(s32[8]{0:T(128)} %fusion.19.order_ref, bf16[544,1024]{1,0:T(8,128)(2,1)} %get-tuple-element.300.x_ref.refs_0_, bf16[544,1024]{1,0:T(8,128)(2,1)} %get-tuple-element.346.refs_1_, bf16[544,4096]{1,0:T(8,128)(2,1)} %get-tuple-element.342.d_ref.refs_2_, ...), custom_call_target="tpu_custom_call" | custom-call | flops 3000000000 | bytes 1 | tf_op jit(solution)/shard_map/pallas_call | solution.py:218
  241.4 14.9 %shard_map.372 = (bf16[1024,3072]{1,0:T(8,128)(2,1)}, f32[16,256]{1,0:T(8,128)}, f32[2,16,128]{2,1,0:T(8,128)}, f32[8,3072]{1,0:T(8,128)}) custom-call(bf16[1024,1024]{1,0:T(8,128)(2,1)} %get-tuple-element.278.q_ref, bf16[1024,1024]{1,0:T(8,128)(2,1)} %get-tuple-element.279.k_ref, bf16[1024,1024]{1,0:T(8,128)(2,1)} %get-tuple-element.280.v_ref, ...), custom_call_target="tpu_custom_call" | custom-call | flops 4200000000 | bytes 1 | tf_op jit(solution)/shard_map/pallas_call | solution.py:453
  259.2 8.7 %shard_map.373 = (bf16[128,3072]{1,0:T(8,128)(2,1)}, bf16[128,3072]{1,0:T(8,128)(2,1)}, bf16[128,3072]{1,0:T(8,128)(2,1)}, bf16[128,3072]{1,0:T(8,128)(2,1)}) custom-call(s32[8]{0:T(128)} %fusion.19.order_ref, bf16[1024,1024]{1,0:T(8,128)(2,1)} %fusion.5.x_ref.refs_0_, bf16[1024,3072]{1,0:T(8,128)(2,1)} %get-tuple-element.439.refs_1_.d_ref), custom_call_target="tpu_custom_call" | custom-call | flops 1800000000 | bytes 1 | tf_op jit(solution)/shard_map/pallas_call | solution.py:218
  270.3 3.9 add_bitcast_fusion
  283.0 9.5 %shard_map.375 = (bf16[2,128,3072]{2,1,0:T(8,128)(2,1)}, bf16[2,128,3072]{2,1,0:T(8,128)(2,1)}) custom-call(s32[8]{0:T(128)} %fusion.19.order_ref, bf16[1024,1024]{1,0:T(8,128)(2,1)} %fusion.5.x_ref.refs_0_, bf16[1024,3072]{1,0:T(8,128)(2,1)} %get-tuple-element.439.refs_1_.d_ref, bf16[128,3072]{1,0:T(8,128)(2,1)} %collective-permute-done.41.refs_2_, ...), custom_call_target="tpu_custom_call" | custom-call | flops 1800000000 | bytes 1 | tf_op jit(solution)/shard_map/pallas_call | solution.py:218
  299.5 12.4 %shard_map.376 = f32[544,1024]{1,0:T(8,128)} custom-call(s32[8]{0:T(128)} %fusion.19.order_ref, bf16[1024,3072]{1,0:T(8,128)(2,1)} %get-tuple-element.439.refs_1_.d_ref, bf16[544,1024]{1,0:T(8,128)(2,1)} %fusion.4.spread_ref, f32[544,1024]{1,0:T(8,128)} %get-tuple-element.440.summed_far, bf16[400,1024]{1,0:T(8,128)(2,1)} %shard_map.358.refs_0_, ...), custom_call_target="tpu_custom_call" | custom-call | flops 3750000128 | bytes 1 | tf_op jit(solution)/shard_map/pallas_call | solution.py:524
  324.0 8.5 %collective-permute-done.55 = bf16[32,5120]{1,0:T(8,128)(2,1)S(1)} collective-permute-done((bf16[32,5120]{1,0:T(8,128)(2,1)S(1)}, bf16[32,5120]{1,0:T(8,128)(2,1)S(1)}, u32[]{:S(2)}, u32[]{:S(2)}) %collective-permute-start.55) | collective-permute-done | bytes 327712 | tf_op jit(solution)/shard_map/ppermute | solution.py:68
  341.5 10.4 %collective-permute-done.58 = bf16[32,5120]{1,0:T(8,128)(2,1)S(1)} collective-permute-done((bf16[32,5120]{1,0:T(8,128)(2,1)S(1)}, bf16[32,5120]{1,0:T(8,128)(2,1)S(1)}, u32[]{:S(2)}, u32[]{:S(2)}) %collective-permute-start.58) | collective-permute-done | bytes 327712 | tf_op jit(solution)/shard_map/ppermute | solution.py:68
  357.7 11.0 %collective-permute-done.60 = bf16[32,3072]{1,0:T(8,128)(2,1)S(1)} collective-permute-done((bf16[32,3072]{1,0:T(8,128)(2,1)S(1)}, bf16[32,3072]{1,0:T(8,128)(2,1)S(1)}, u32[]{:S(2)}, u32[]{:S(2)}) %collective-permute-start.60) | collective-permute-done | bytes 196640 | tf_op jit(solution)/shard_map/ppermute | solution.py:68
  377.1 4.7 %collective-permute-done.63 = bf16[32,3072]{1,0:T(8,128)(2,1)S(1)} collective-permute-done((bf16[32,3072]{1,0:T(8,128)(2,1)S(1)}, bf16[32,3072]{1,0:T(8,128)(2,1)S(1)}, u32[]{:S(2)}, u32[]{:S(2)}) %collective-permute-start.63) | collective-permute-done | bytes 196640 | tf_op jit(solution)/shard_map/ppermute | solution.py:68
  (259 shorter events, 127.5 us)
Async XLA Ops:
  3.6 21.9 %collective-permute-start = (bf16[400,1024]{1,0:T(8,128)(2,1)}, bf16[400,1024]{1,0:T(8,128)(2,1)S(1)}, u32[]{:S(2)}, u32[]{:S(2)}) collective-permute-start(bf16[400,1024]{1,0:T(8,128)(2,1)} %shard_map.358.refs_0_), channel_id=1, source_target_pairs={{0,16},{4,12},{8,24},{12,4},{16,0},{20,28},{24,8},{28,20},{1,17},{... | collective-permute-start | bytes 2457608 | tf_op jit(solution)/shard_map/ppermute | solution.py:56
  6.6 18.9 %collective-permute-start.1 = (bf16[400,1024]{1,0:T(8,128)(2,1)}, bf16[400,1024]{1,0:T(8,128)(2,1)S(1)}, u32[]{:S(2)}, u32[]{:S(2)}) collective-permute-start(bf16[400,1024]{1,0:T(8,128)(2,1)} %shard_map.358.refs_0_), channel_id=1, source_target_pairs={{0,8},{4,20},{8,0},{12,28},{16,24},{20,4},{24,16},{28,12},{1,9},{5... | collective-permute-start | bytes 2457608 | tf_op jit(solution)/shard_map/ppermute | solution.py:56
  25.5 24.1 %collective-permute-start.6 = (bf16[128,4096]{1,0:T(8,128)(2,1)}, bf16[128,4096]{1,0:T(8,128)(2,1)}, u32[]{:S(2)}, u32[]{:S(2)}) collective-permute-start(bf16[128,4096]{1,0:T(8,128)(2,1)} %refs_0_.6), channel_id=1, source_target_pairs={{0,16},{4,12},{8,24},{12,4},{16,0},{20,28},{24,8},{28,20},{1,17},{... | collective-permute-start | bytes 3145736 | tf_op jit(solution)/shard_map/ppermute | solution.py:56
  27.9 20.7 %collective-permute-start.2 = (bf16[400,1024]{1,0:T(8,128)(2,1)S(1)}, bf16[400,1024]{1,0:T(8,128)(2,1)}, u32[]{:S(2)}, u32[]{:S(2)}) collective-permute-start(bf16[400,1024]{1,0:T(8,128)(2,1)S(1)} %collective-permute-done.refs_1_), channel_id=1, source_target_pairs={{0,8},{4,20},{8,0},{12,28},{16,24},{20,4},{24,16},{28,12},{1,9},{5... | collective-permute-start | bytes 2457608 | tf_op jit(solution)/shard_map/ppermute | solution.py:56
  28.6 20.0 %collective-permute-start.4 = (bf16[400,1024]{1,0:T(8,128)(2,1)S(1)}, bf16[400,1024]{1,0:T(8,128)(2,1)S(1)}, u32[]{:S(2)}, u32[]{:S(2)}) collective-permute-start(bf16[400,1024]{1,0:T(8,128)(2,1)S(1)} %collective-permute-done.refs_1_), channel_id=1, source_target_pairs={{0,4},{4,0},{8,12},{12,8},{16,20},{20,16},{24,28},{28,24},{1,5},{5... | collective-permute-start | bytes 2457608 | tf_op jit(solution)/shard_map/ppermute | solution.py:56
  28.6 20.0 %collective-permute-start.3 = (bf16[400,1024]{1,0:T(8,128)(2,1)S(1)}, bf16[400,1024]{1,0:T(8,128)(2,1)S(1)}, u32[]{:S(2)}, u32[]{:S(2)}) collective-permute-start(bf16[400,1024]{1,0:T(8,128)(2,1)S(1)} %copy-done.4), channel_id=1, source_target_pairs={{0,4},{4,0},{8,12},{12,8},{16,20},{20,16},{24,28},{28,24},{1,5},{5... | collective-permute-start | bytes 2457608 | tf_op jit(solution)/shard_map/ppermute | solution.py:56
  29.1 19.6 %collective-permute-start.5 = (bf16[400,1024]{1,0:T(8,128)(2,1)S(1)}, bf16[400,1024]{1,0:T(8,128)(2,1)S(1)}, u32[]{:S(2)}, u32[]{:S(2)}) collective-permute-start(bf16[400,1024]{1,0:T(8,128)(2,1)S(1)} %collective-permute-done.1.refs_2_), channel_id=1, source_target_pairs={{0,4},{4,0},{8,12},{12,8},{16,20},{20,16},{24,28},{28,24},{1,5},{5... | collective-permute-start | bytes 2457608 | tf_op jit(solution)/shard_map/ppermute | solution.py:56
  50.5 20.9 %collective-permute-start.8 = (bf16[128,4096]{1,0:T(8,128)(2,1)}, bf16[128,4096]{1,0:T(8,128)(2,1)}, u32[]{:S(2)}, u32[]{:S(2)}) collective-permute-start(bf16[128,4096]{1,0:T(8,128)(2,1)} %refs_0_.6), channel_id=1, source_target_pairs={{0,8},{4,20},{8,0},{12,28},{16,24},{20,4},{24,16},{28,12},{1,9},{5... | collective-permute-start | bytes 3145736 | tf_op jit(solution)/shard_map/ppermute | solution.py:56
  51.3 20.1 %collective-permute-start.10 = (bf16[128,1024]{1,0:T(8,128)(2,1)S(1)}, bf16[128,1024]{1,0:T(8,128)(2,1)}, u32[]{:S(2)}, u32[]{:S(2)}) collective-permute-start(bf16[128,1024]{1,0:T(8,128)(2,1)S(1)} %copy-done.25), channel_id=1, source_target_pairs={{0,8},{4,20},{8,0},{12,28},{16,24},{20,4},{24,16},{28,12},{1,9},{5... | collective-permute-start | bytes 786440 | tf_op jit(solution)/shard_map/ppermute | solution.py:56
  53.1 18.3 %collective-permute-start.9 = (bf16[128,1024]{1,0:T(8,128)(2,1)S(1)}, bf16[128,1024]{1,0:T(8,128)(2,1)}, u32[]{:S(2)}, u32[]{:S(2)}) collective-permute-start(bf16[128,1024]{1,0:T(8,128)(2,1)S(1)} %copy-done.25), channel_id=1, source_target_pairs={{0,16},{4,12},{8,24},{12,4},{16,0},{20,28},{24,8},{28,20},{1,17},{... | collective-permute-start | bytes 786440 | tf_op jit(solution)/shard_map/ppermute | solution.py:56
  71.4 17.2 %collective-permute-start.11 = (bf16[512,1024]{1,0:T(8,128)(2,1)S(1)}, bf16[512,1024]{1,0:T(8,128)(2,1)}, u32[]{:S(2)}, u32[]{:S(2)}) collective-permute-start(bf16[512,1024]{1,0:T(8,128)(2,1)S(1)} %copy-done), channel_id=1, source_target_pairs={{0,16},{4,12},{8,24},{12,4},{16,0},{20,28},{24,8},{28,20},{1,17},{... | collective-permute-start | bytes 3145736 | tf_op jit(solution)/shard_map/ppermute | solution.py:56
  91.2 25.4 %collective-permute-start.17 = (bf16[128,4096]{1,0:T(8,128)(2,1)}, bf16[128,4096]{1,0:T(8,128)(2,1)}, u32[]{:S(2)}, u32[]{:S(2)}) collective-permute-start(bf16[128,4096]{1,0:T(8,128)(2,1)} %collective-permute-done.6.refs_1_), channel_id=1, source_target_pairs={{0,8},{4,20},{8,0},{12,28},{16,24},{20,4},{24,16},{28,12},{1,9},{5... | collective-permute-start | bytes 3145736 | tf_op jit(solution)/shard_map/ppermute | solution.py:56
  92.5 24.1 %collective-permute-start.19 = (bf16[128,4096]{1,0:T(8,128)(2,1)}, bf16[128,4096]{1,0:T(8,128)(2,1)}, u32[]{:S(2)}, u32[]{:S(2)}) collective-permute-start(bf16[128,4096]{1,0:T(8,128)(2,1)} %collective-permute-done.6.refs_1_), channel_id=1, source_target_pairs={{0,4},{4,0},{8,12},{12,8},{16,20},{20,16},{24,28},{28,24},{1,5},{5... | collective-permute-start | bytes 3145736 | tf_op jit(solution)/shard_map/ppermute | solution.py:56
  92.5 24.1 %collective-permute-start.20 = (bf16[128,4096]{1,0:T(8,128)(2,1)}, bf16[128,4096]{1,0:T(8,128)(2,1)}, u32[]{:S(2)}, u32[]{:S(2)}) collective-permute-start(bf16[128,4096]{1,0:T(8,128)(2,1)} %collective-permute-done.8.refs_2_), channel_id=1, source_target_pairs={{0,4},{4,0},{8,12},{12,8},{16,20},{20,16},{24,28},{28,24},{1,5},{5... | collective-permute-start | bytes 3145736 | tf_op jit(solution)/shard_map/ppermute | solution.py:56
  184.8 26.4 %collective-permute-start.32 = (bf16[2,1024,512]{2,1,0:T(8,128)(2,1)}, bf16[2,1024,512]{2,1,0:T(8,128)(2,1)}, u32[]{:S(2)}, u32[]{:S(2)}) collective-permute-start(bf16[2,1024,512]{2,1,0:T(8,128)(2,1)} %get-tuple-element.352), channel_id=1, source_target_pairs={{0,8},{4,20},{8,0},{12,28},{16,24},{20,4},{24,16},{28,12},{1,9},{5... | collective-permute-start | bytes 6291464 | tf_op jit(solution)/shard_map/ppermute | solution.py:56
  215.6 20.7 %collective-permute-start.37 = (bf16[1024,512]{1,0:T(8,128)(2,1)}, bf16[1024,512]{1,0:T(8,128)(2,1)}, u32[]{:S(2)}, u32[]{:S(2)}) collective-permute-start(bf16[1024,512]{1,0:T(8,128)(2,1)} %get-tuple-element.540), channel_id=1, source_target_pairs={{0,16},{4,12},{8,24},{12,4},{16,0},{20,28},{24,8},{28,20},{1,17},{... | collective-permute-start | bytes 3145736 | tf_op jit(solution)/shard_map/ppermute | solution.py:56
  236.2 34.1 %collective-permute-start.40 = (bf16[2,128,5120]{2,1,0:T(8,128)(2,1)}, bf16[2,128,5120]{2,1,0:T(8,128)(2,1)}, u32[]{:S(2)}, u32[]{:S(2)}) collective-permute-start(bf16[2,128,5120]{2,1,0:T(8,128)(2,1)} %get-tuple-element.390), channel_id=1, source_target_pairs={{0,8},{4,20},{8,0},{12,28},{16,24},{20,4},{24,16},{28,12},{1,9},{5... | collective-permute-start | bytes 7864328 | tf_op jit(solution)/shard_map/ppermute | solution.py:56
  239.5 16.8 %collective-permute-start.38 = (bf16[512,512]{1,0:T(8,128)(2,1)S(1)}, bf16[512,512]{1,0:T(8,128)(2,1)S(1)}, u32[]{:S(2)}, u32[]{:S(2)}) collective-permute-start(bf16[512,512]{1,0:T(8,128)(2,1)S(1)} %get-tuple-element.553), channel_id=1, source_target_pairs={{0,1},{1,0},{2,3},{3,2},{4,5},{5,4},{6,7},{7,6},{8,9},{9,8},{10,11... | collective-permute-start | bytes 1572872 | tf_op jit(solution)/shard_map/ppermute | solution.py:68
  274.2 19.1 %collective-permute-start.45 = (bf16[128,5120]{1,0:T(8,128)(2,1)}, bf16[128,5120]{1,0:T(8,128)(2,1)}, u32[]{:S(2)}, u32[]{:S(2)}) collective-permute-start(bf16[128,5120]{1,0:T(8,128)(2,1)} %get-tuple-element.538), channel_id=1, source_target_pairs={{0,16},{4,12},{8,24},{12,4},{16,0},{20,28},{24,8},{28,20},{1,17},{... | collective-permute-start | bytes 3932168 | tf_op jit(solution)/shard_map/ppermute | solution.py:56
  293.3 20.7 %collective-permute-start.47 = (bf16[2,128,3072]{2,1,0:T(8,128)(2,1)}, bf16[2,128,3072]{2,1,0:T(8,128)(2,1)}, u32[]{:S(2)}, u32[]{:S(2)}) collective-permute-start(bf16[2,128,3072]{2,1,0:T(8,128)(2,1)} %get-tuple-element.438), channel_id=1, source_target_pairs={{0,8},{4,20},{8,0},{12,28},{16,24},{20,4},{24,16},{28,12},{1,9},{5... | collective-permute-start | bytes 4718600 | tf_op jit(solution)/shard_map/ppermute | solution.py:56
  314.1 20.1 %collective-permute-start.56 = (bf16[512,512]{1,0:T(8,128)(2,1)S(1)}, bf16[512,512]{1,0:T(8,128)(2,1)S(1)}, u32[]{:S(2)}, u32[]{:S(2)}) collective-permute-start(bf16[512,512]{1,0:T(8,128)(2,1)S(1)} %pad_maximum_fusion.1), channel_id=1, source_target_pairs={{0,1},{1,0},{2,3},{3,2},{4,5},{5,4},{6,7},{7,6},{8,9},{9,8},{10,11... | collective-permute-start | bytes 1572872 | tf_op jit(solution)/shard_map/ppermute | solution.py:68
  316.7 17.5 %collective-permute-start.53 = (bf16[128,3072]{1,0:T(8,128)(2,1)S(1)}, bf16[128,3072]{1,0:T(8,128)(2,1)S(1)}, u32[]{:S(2)}, u32[]{:S(2)}) collective-permute-start(bf16[128,3072]{1,0:T(8,128)(2,1)S(1)} %get-tuple-element.542), channel_id=1, source_target_pairs={{0,16},{4,12},{8,24},{12,4},{16,0},{20,28},{24,8},{28,20},{1,17},{... | collective-permute-start | bytes 2359304 | tf_op jit(solution)/shard_map/ppermute | solution.py:56
  334.5 17.4 %collective-permute-start.57 = (bf16[64,3072]{1,0:T(8,128)(2,1)S(1)}, bf16[64,3072]{1,0:T(8,128)(2,1)S(1)}, u32[]{:S(2)}, u32[]{:S(2)}) collective-permute-start(bf16[64,3072]{1,0:T(8,128)(2,1)S(1)} %get-tuple-element.557), channel_id=1, source_target_pairs={{0,1},{1,0},{2,3},{3,2},{4,5},{5,4},{6,7},{7,6},{8,9},{9,8},{10,11... | collective-permute-start | bytes 1179656 | tf_op jit(solution)/shard_map/ppermute | solution.py:68
  352.6 17.9 %collective-permute-start.61 = (bf16[64,5120]{1,0:T(8,128)(2,1)S(1)}, bf16[64,5120]{1,0:T(8,128)(2,1)S(1)}, u32[]{:S(2)}, u32[]{:S(2)}) collective-permute-start(bf16[64,5120]{1,0:T(8,128)(2,1)S(1)} %pad_maximum_fusion), channel_id=1, source_target_pairs={{0,1},{1,0},{2,3},{3,2},{4,5},{5,4},{6,7},{7,6},{8,9},{9,8},{10,11... | collective-permute-start | bytes 1966088 | tf_op jit(solution)/shard_map/ppermute | solution.py:68
  (77 other events, 690.5 us)
where the time goes:
time: 399 us; the launch traced here: 394 us
  Pallas kernels  197 us (49%)
  waiting for transfers between devices  104 us (26%)
  starting transfers between devices  50 us (13%)
  other arithmetic  20.4 us (5%)
  local copies, waits for them, and re-layouts  14.4 us (4%)
  matrix products  5.95 us (1%)
    pallas_call x8, Pallas kernels, run(): pl.pallas_call(kernel, out_shape=tuple((jax.ShapeDtypeStruct(item[0], ite...  98.5 us
    ppermute x52, waiting for transfers between devices, hop(): return lax.ppermute(value, 'fsdp', pairs)  54.7 us
    ppermute x14, waiting for transfers between devices, trade(): return lax.ppermute(value, 'dp', [(i, i ^ bit) for i in range(4)])  49.5 us
    pallas_call x4, Pallas kernels, grad_blocks(): pl.pallas_call(partial(grad_kernel, first, tuple(counts), fold), grid_spe...  39.9 us
    ppermute x52, starting transfers between devices, hop(): return lax.ppermute(value, 'fsdp', pairs)  30.5 us
    pallas_call x2, Pallas kernels, turned_blocks(): pl.pallas_call(partial(turned_kernel, fold), grid_spec=pltpu.PrefetchScal...  19.6 us
    ppermute x14, starting transfers between devices, trade(): return lax.ppermute(value, 'dp', [(i, i ^ bit) for i in range(4)])  19.5 us
    pallas_call x1, Pallas kernels, attend_back(): pl.pallas_call(attend_back_kernel, grid=(PAGES,), in_specs=[wide, wide, w...  14.9 us
  transfers between devices with their start and end apart: 66, of which 24 were waited for; matrix products, arithmetic and copies ran while one was open for 7% of the time, Pallas kernels for 40%

commit v1 on v0

--- a/solution.py
+++ b/solution.py
@@ -123,49 +123,59 @@
         outs[k][...] = found.astype(BF)
 
 
-def turned_kernel(fold, order_ref, left_ref, right_ref, *refs):
-    others, outs, turned = refs[: 4 * fold], refs[4 * fold : -1], refs[-1]
-    i = pl.program_id(0)
-
-    @pl.when(i == 0)
-    def _():
-        turned[...] = right_ref[...].T
-
-    found = dot(turned[...], left_ref[...])
+def turned_kernel(first, fold, order_ref, right_ref, left_far, *refs):
+    others, outs = refs[: 4 * fold], refs[4 * fold : -7]
+    lefts, turned, came, left, in_sem, other_sem, out_sem = refs[-7:]
+    rows = lefts.shape[2]
+    copies = [
+        begin(left_far.at[:, lanes(order_ref, first + k, rows)], lefts.at[k], in_sem.at[k])
+        for k in range(4)
+    ]
+    arrivals = [begin(others[k], came.at[k], other_sem.at[k]) for k in range(4 * fold)]
+    turned[...] = right_ref[...].T
+    leaving = []
     for k in range(4):
-
-        @pl.when(i == k)
-        def _():
-            emit(found, k, others, outs)
+        copies[k].wait()
+        found = dot(turned[...], lefts[k])
+        if fold:
+            arrivals[k].wait()
+            found = found + came[k].astype(F32)
+        left[k] = found.astype(BF)
+        target = outs[k // 2].at[k % 2] if fold else outs[k]
+        leaving.append(begin(left.at[k], target, out_sem.at[k]))
+    finish(leaving)
 
 
 def turned_blocks(order, first, left, right, others=()):
     depth, rows, columns = left.shape[0], left.shape[1] // 8, right.shape[1]
     fold = int(bool(others))
-    whole = pl.BlockSpec((columns, rows), lambda i, n: (0, 0))
+    far = pl.BlockSpec(memory_space=pltpu.HBM)
     if fold:
-        out_specs = (pl.BlockSpec((2, columns, rows), lambda i, n: (0, 0, 0)),) * 2
         shapes = (jax.ShapeDtypeStruct((2, columns, rows), BF),) * 2
     else:
-        out_specs = (whole,) * 4
         shapes = (jax.ShapeDtypeStruct((columns, rows), BF),) * 4
     return pl.pallas_call(
-        partial(turned_kernel, fold),
-        grid_spec=pltpu.PrefetchScalarGridSpec(
-            num_scalar_prefetch=1,
-            grid=(4,),
-            in_specs=[
-                pl.BlockSpec((depth, rows), lambda i, n: (0, n[first + i])),
-                pl.BlockSpec((depth, columns), lambda i, n: (0, 0)),
-            ]
-            + [whole] * (4 * fold),
-            out_specs=out_specs,
-            scratch_shapes=[pltpu.VMEM((columns, depth), left.dtype)],
-        ),
+        partial(turned_kernel, first, fold),
         out_shape=shapes,
+        in_specs=[
+            pl.BlockSpec(memory_space=pltpu.SMEM),
+            pl.BlockSpec(memory_space=pltpu.VMEM),
+            far,
+        ]
+        + [far] * (4 * fold),
+        out_specs=(far,) * len(shapes),
+        scratch_shapes=[
+            pltpu.VMEM((4, depth, rows), BF),
+            pltpu.VMEM((columns, depth), BF),
+            pltpu.VMEM((4, columns, rows) if fold else (1, 16, 128), BF),
+            pltpu.VMEM((4, columns, rows), BF),
+            pltpu.SemaphoreType.DMA((4,)),
+            pltpu.SemaphoreType.DMA((4,)),
+            pltpu.SemaphoreType.DMA((4,)),
+        ],
         compiler_params=pltpu.CompilerParams(vmem_limit_bytes=VMEM_LIMIT),
         cost_estimate=cost(7),
-    )(order, left, right, *others)
+    )(order, right, left, *others)
 
 
 def grad_kernel(first, counts, fold, order_ref, *refs):
@@ -546,10 +556,9 @@
 
 
 def each_rows(group, body, carry):
-    def step(c, carry):
-        return body(pl.ds(pl.multiple_of(c * ROWS_AT_ONCE, ROWS_AT_ONCE), ROWS_AT_ONCE), carry)
-
-    return lax.fori_loop(group[0], group[-1] + 1, step, carry)
+    for c in group:
+        carry = body(pl.ds(c * ROWS_AT_ONCE, ROWS_AT_ONCE), carry)
+    return carry
 
 
 def row_groups(count):

time: 399 us -> 393 us (0.985)
  Pallas kernels: 197 us -> 187 us
    pallas_call x8, Pallas kernels: 98.5 us -> 92.2 us  [run(): pl.pallas_call(kernel, out_shape=tuple((jax.ShapeDtypeStruct(item[0], ite...]
    pallas_call x2, Pallas kernels: 19.6 us -> 15.4 us  [turned_blocks(): pl.pallas_call(partial(turned_kernel, first, fold), out_shape=shapes, in_...]
  transfers between devices with their start and end apart: 66 -> 66, of which waited for: 24 -> 26; matrix products, arithmetic and copies ran while one was open for 7% -> 7% of each run, Pallas kernels for 40% -> 40%
where the time goes in v1:
time: 393 us; the launch traced here: 387 us
  Pallas kernels  187 us (48%)
  waiting for transfers between devices  106 us (27%)
  starting transfers between devices  52.3 us (13%)
  other arithmetic  20.4 us (5%)
  local copies, waits for them, and re-layouts  14.4 us (4%)
  matrix products  5.95 us (2%)
    pallas_call x8, Pallas kernels, run(): pl.pallas_call(kernel, out_shape=tuple((jax.ShapeDtypeStruct(item[0], ite...  92.2 us
    ppermute x52, waiting for transfers between devices, hop(): return lax.ppermute(value, 'fsdp', pairs)  58.1 us
    ppermute x14, waiting for transfers between devices, trade(): return lax.ppermute(value, 'dp', [(i, i ^ bit) for i in range(4)])  47.7 us
    pallas_call x4, Pallas kernels, grad_blocks(): pl.pallas_call(partial(grad_kernel, first, tuple(counts), fold), grid_spe...  40.5 us
    ppermute x52, starting transfers between devices, hop(): return lax.ppermute(value, 'fsdp', pairs)  30.5 us
    ppermute x14, starting transfers between devices, trade(): return lax.ppermute(value, 'dp', [(i, i ^ bit) for i in range(4)])  21.8 us
    pallas_call x2, Pallas kernels, turned_blocks(): pl.pallas_call(partial(turned_kernel, first, fold), out_shape=shapes, in_...  15.4 us
    pallas_call x1, Pallas kernels, attend_back(): pl.pallas_call(attend_back_kernel, grid=(PAGES,), in_specs=[wide, wide, w...  14.7 us
  transfers between devices with their start and end apart: 66, of which 26 were waited for; matrix products, arithmetic and copies ran while one was open for 7% of the time, Pallas kernels for 40%

profile of v1, /device:TPU:0, one launch (start us, length us, event | category | flops | bytes accessed | tf_op | source)
XLA Modules:
  0.0 387.2 jit_solution(2200257517249610840)
XLA Ops:
  17.7 7.7 %collective-permute-done.refs_1_ = bf16[400,1024]{1,0:T(8,128)(2,1)S(1)} collective-permute-done((bf16[400,1024]{1,0:T(8,128)(2,1)}, bf16[400,1024]{1,0:T(8,128)(2,1)S(1)}, u32[]{:S(2)}, u32[]{:S(2)}) %collective-permute-start) | collective-permute-done | bytes 819232 | tf_op jit(solution)/shard_map/ppermute | solution.py:56
  29.1 19.5 %collective-permute-done.2.refs_3_ = bf16[400,1024]{1,0:T(8,128)(2,1)} collective-permute-done((bf16[400,1024]{1,0:T(8,128)(2,1)S(1)}, bf16[400,1024]{1,0:T(8,128)(2,1)}, u32[]{:S(2)}, u32[]{:S(2)}) %collective-permute-start.2) | collective-permute-done | bytes 819232 | tf_op jit(solution)/shard_map/ppermute | solution.py:56
  54.6 13.0 %shard_map.359 = (bf16[1024,1024]{1,0:T(8,128)(2,1)}, bf16[1024,1024]{1,0:T(8,128)(2,1)}, bf16[1024,1024]{1,0:T(8,128)(2,1)}, f32[16,4096]{1,0:T(8,128)}, f32[48,1,128]{2,1,0:T(1,128)}) custom-call(s32[8]{0:T(128)} %fusion.19.order_ref, bf16[1024,1024]{1,0:T(8,128)(2,1)} %fusion.5.x_ref.refs_0_, bf16[400,1024]{1,0:T(8,128)(2,1)} %shard_map.358.refs_0_, ...), custom_call_target="tpu_custom_call" | custom-call | flops 3600000000 | bytes 1 | tf_op jit(solution)/shard_map/pallas_call | solution.py:534
  73.3 14.5 %shard_map.361 = (bf16[1024,1024]{1,0:T(8,128)(2,1)}, bf16[8,8,128,256]{3,2,1,0:T(8,128)(2,1)}) custom-call(s32[8]{0:T(128)} %get-tuple-element.536.length_ref, bf16[1024,1024]{1,0:T(8,128)(2,1)} %get-tuple-element.278.q_ref, bf16[1024,1024]{1,0:T(8,128)(2,1)} %get-tuple-element.279.k_ref, bf16[1024,1024]{1,0:T(8,128)(2,1)} %get-tuple-element.280.v_ref, ...), custom_call_target="tpu_custom_call" | custom-call | flops 4050000128 | bytes 1 | tf_op jit(solution)/shard_map/pallas_call | solution.py:352
  93.4 9.0 %shard_map.362 = (bf16[544,1024]{1,0:T(8,128)(2,1)}, f32[544,1024]{1,0:T(8,128)}, f32[544,1]{1,0:T(8,128)}, bf16[544,1024]{1,0:T(8,128)(2,1)}) custom-call(s32[8]{0:T(128)} %fusion.19.order_ref, bf16[1024,1024]{1,0:T(8,128)(2,1)} %get-tuple-element.290.c_ref, bf16[544,1024]{1,0:T(8,128)(2,1)} %fusion.4.spread_ref, bf16[544,1024]{1,0:T(8,128)(2,1)} %hidden_ref.1, ...), custom_call_target="tpu_custom_call" | custom-call | flops 2100000000 | bytes 1 | tf_op jit(solution)/shard_map/pallas_call | solution.py:534
  105.4 11.2 %collective-permute-done.17.refs_3_ = bf16[128,4096]{1,0:T(8,128)(2,1)} collective-permute-done((bf16[128,4096]{1,0:T(8,128)(2,1)}, bf16[128,4096]{1,0:T(8,128)(2,1)}, u32[]{:S(2)}, u32[]{:S(2)}) %collective-permute-start.17) | collective-permute-done | bytes 1048608 | tf_op jit(solution)/shard_map/ppermute | solution.py:56
  120.4 12.4 %shard_map.363 = (bf16[544,4096]{1,0:T(8,128)(2,1)}, bf16[544,4096]{1,0:T(8,128)(2,1)}) custom-call(s32[8]{0:T(128)} %fusion.19.order_ref, bf16[544,1024]{1,0:T(8,128)(2,1)} %get-tuple-element.300.x_ref.refs_0_, f32[16,4096]{1,0:T(8,128)} %get-tuple-element.268.vector_ref, bf16[128,4096]{1,0:T(8,128)(2,1)} %refs_0_.6, ...), custom_call_target="tpu_custom_call" | custom-call | flops 4200000000 | bytes 1 | tf_op jit(solution)/shard_map/pallas_call | solution.py:534
  136.7 13.2 %shard_map.364 = (bf16[544,1024]{1,0:T(8,128)(2,1)}, f32[544,1024]{1,0:T(8,128)}, bf16[544,1024]{1,0:T(8,128)(2,1)}, f32[8,1024]{1,0:T(8,128)}) custom-call(s32[8]{0:T(128)} %fusion.19.order_ref, f32[16,4096]{1,0:T(8,128)} %get-tuple-element.268.vector_ref, bf16[544,4096]{1,0:T(8,128)(2,1)} %get-tuple-element.311.a_far.left_far, ...), custom_call_target="tpu_custom_call" | custom-call | flops 3449999872 | bytes 1 | tf_op jit(solution)/shard_map/pallas_call | solution.py:534
  149.9 7.3 %shard_map.365 = (bf16[1024,512]{1,0:T(8,128)(2,1)}, bf16[1024,512]{1,0:T(8,128)(2,1)}, bf16[1024,512]{1,0:T(8,128)(2,1)}, bf16[1024,512]{1,0:T(8,128)(2,1)}) custom-call(s32[8]{0:T(128)} %fusion.19.order_ref, bf16[544,1024]{1,0:T(8,128)(2,1)} %get-tuple-element.326.right_ref.d_ref, bf16[544,4096]{1,0:T(8,128)(2,1)} %get-tuple-element.311.a_far.left_far), custom_call_target="tpu_custom_call" | custom-call | flops 2100000000 | bytes 1 | tf_op jit(solution)/shard_map/pallas_call | solution.py:157
  158.3 10.8 %shard_map.366 = (bf16[544,4096]{1,0:T(8,128)(2,1)}, f32[8,4096]{1,0:T(8,128)}) custom-call(s32[8]{0:T(128)} %fusion.19.order_ref, bf16[544,1024]{1,0:T(8,128)(2,1)} %get-tuple-element.326.right_ref.d_ref, bf16[544,4096]{1,0:T(8,128)(2,1)} %get-tuple-element.327.steep_far, bf16[512,1024]{1,0:T(8,128)(2,1)} %refs_0_.5, ...), custom_call_target="tpu_custom_call" | custom-call | flops 3000000000 | bytes 1 | tf_op jit(solution)/shard_map/pallas_call | solution.py:534
  170.1 8.1 %shard_map.367 = (bf16[2,1024,512]{2,1,0:T(8,128)(2,1)}, bf16[2,1024,512]{2,1,0:T(8,128)(2,1)}) custom-call(s32[8]{0:T(128)} %fusion.19.order_ref, bf16[544,1024]{1,0:T(8,128)(2,1)} %get-tuple-element.326.right_ref.d_ref, bf16[544,4096]{1,0:T(8,128)(2,1)} %get-tuple-element.311.a_far.left_far, bf16[1024,512]{1,0:T(8,128)(2,1)} %copy-done.3, ...), custom_call_target="tpu_custom_call" | custom-call | flops 2100000000 | bytes 1 | tf_op jit(solution)/shard_map/pallas_call | solution.py:157
  179.0 12.9 %shard_map.368 = (f32[544,1024]{1,0:T(8,128)}, bf16[544,1024]{1,0:T(8,128)(2,1)}, f32[8,1024]{1,0:T(8,128)}) custom-call(s32[8]{0:T(128)} %fusion.19.order_ref, bf16[544,4096]{1,0:T(8,128)(2,1)} %get-tuple-element.342.d_ref.refs_2_, f32[544,1]{1,0:T(8,128)} %get-tuple-element.343.deviation_ref, f32[16,4096]{1,0:T(8,128)} %get-tuple-element.268.vector_ref, ...), custom_call_target="tpu_custom_call" | custom-call | flops 4800000000 | bytes 1 | tf_op jit(solution)/shard_map/pallas_call | solution.py:534
  191.9 10.7 %shard_map.369 = (bf16[128,5120]{1,0:T(8,128)(2,1)}, bf16[128,5120]{1,0:T(8,128)(2,1)}, bf16[128,5120]{1,0:T(8,128)(2,1)}, bf16[128,5120]{1,0:T(8,128)(2,1)}) custom-call(s32[8]{0:T(128)} %fusion.19.order_ref, bf16[544,1024]{1,0:T(8,128)(2,1)} %get-tuple-element.300.x_ref.refs_0_, bf16[544,1024]{1,0:T(8,128)(2,1)} %get-tuple-element.346.refs_1_, ...), custom_call_target="tpu_custom_call" | custom-call | flops 3000000000 | bytes 1 | tf_op jit(solution)/shard_map/pallas_call | solution.py:228
  209.8 8.5 %shard_map.370.g_ref = bf16[1024,1024]{1,0:T(8,128)(2,1)} custom-call(s32[8]{0:T(128)} %fusion.19.order_ref, bf16[544,1024]{1,0:T(8,128)(2,1)} %get-tuple-element.353.refs_3_.d_ref, bf16[1024,544]{1,0:T(8,128)(2,1)} %fusion.spread_ref, bf16[128,1024]{1,0:T(8,128)(2,1)} %refs_0_.7, bf16[128,1024]{1,0:T(8,128)(2,1)} %collective-permute-done.9.refs_1_, ...), custom_call_target="tpu_custom_call" | custom-call | flops 1950000000 | bytes 1 | tf_op jit(solution)/shard_map/pallas_call | solution.py:534
  218.3 11.4 %shard_map.371 = (bf16[2,128,5120]{2,1,0:T(8,128)(2,1)}, bf16[2,128,5120]{2,1,0:T(8,128)(2,1)}) custom-call(s32[8]{0:T(128)} %fusion.19.order_ref, bf16[544,1024]{1,0:T(8,128)(2,1)} %get-tuple-element.300.x_ref.refs_0_, bf16[544,1024]{1,0:T(8,128)(2,1)} %get-tuple-element.346.refs_1_, bf16[544,4096]{1,0:T(8,128)(2,1)} %get-tuple-element.342.d_ref.refs_2_, ...), custom_call_target="tpu_custom_call" | custom-call | flops 3000000000 | bytes 1 | tf_op jit(solution)/shard_map/pallas_call | solution.py:228
  234.8 14.7 %shard_map.372 = (bf16[1024,3072]{1,0:T(8,128)(2,1)}, f32[16,256]{1,0:T(8,128)}, f32[2,16,128]{2,1,0:T(8,128)}, f32[8,3072]{1,0:T(8,128)}) custom-call(bf16[1024,1024]{1,0:T(8,128)(2,1)} %get-tuple-element.278.q_ref, bf16[1024,1024]{1,0:T(8,128)(2,1)} %get-tuple-element.279.k_ref, bf16[1024,1024]{1,0:T(8,128)(2,1)} %get-tuple-element.280.v_ref, ...), custom_call_target="tpu_custom_call" | custom-call | flops 4200000000 | bytes 1 | tf_op jit(solution)/shard_map/pallas_call | solution.py:463
  252.3 8.7 %shard_map.373 = (bf16[128,3072]{1,0:T(8,128)(2,1)}, bf16[128,3072]{1,0:T(8,128)(2,1)}, bf16[128,3072]{1,0:T(8,128)(2,1)}, bf16[128,3072]{1,0:T(8,128)(2,1)}) custom-call(s32[8]{0:T(128)} %fusion.19.order_ref, bf16[1024,1024]{1,0:T(8,128)(2,1)} %fusion.5.x_ref.refs_0_, bf16[1024,3072]{1,0:T(8,128)(2,1)} %get-tuple-element.439.refs_1_.d_ref), custom_call_target="tpu_custom_call" | custom-call | flops 1800000000 | bytes 1 | tf_op jit(solution)/shard_map/pallas_call | solution.py:228
  263.5 3.9 %add_bitcast_fusion = (bf16[128,5120]{1,0:T(8,128)(2,1)}, bf16[128,5120]{1,0:T(8,128)(2,1)S(1)}) fusion(bf16[2,128,5120]{2,1,0:T(8,128)(2,1)} %collective-permute-done.40, bf16[2,128,5120]{2,1,0:T(8,128)(2,1)} %get-tuple-element.416), kind=kLoop, calls=%fused_computation.10 | loop fusion | flops 1310720 | bytes 7864320 | tf_op jit(solution)/shard_map/add | solution.py:64
  276.4 9.7 %shard_map.375 = (bf16[2,128,3072]{2,1,0:T(8,128)(2,1)}, bf16[2,128,3072]{2,1,0:T(8,128)(2,1)}) custom-call(s32[8]{0:T(128)} %fusion.19.order_ref, bf16[1024,1024]{1,0:T(8,128)(2,1)} %fusion.5.x_ref.refs_0_, bf16[1024,3072]{1,0:T(8,128)(2,1)} %get-tuple-element.439.refs_1_.d_ref, bf16[128,3072]{1,0:T(8,128)(2,1)} %collective-permute-done.41.refs_2_, ...), custom_call_target="tpu_custom_call" | custom-call | flops 1800000000 | bytes 1 | tf_op jit(solution)/shard_map/pallas_call | solution.py:228
  292.8 12.4 %shard_map.376 = f32[544,1024]{1,0:T(8,128)} custom-call(s32[8]{0:T(128)} %fusion.19.order_ref, bf16[1024,3072]{1,0:T(8,128)(2,1)} %get-tuple-element.439.refs_1_.d_ref, bf16[544,1024]{1,0:T(8,128)(2,1)} %fusion.4.spread_ref, f32[544,1024]{1,0:T(8,128)} %get-tuple-element.440.summed_far, bf16[400,1024]{1,0:T(8,128)(2,1)} %shard_map.358.refs_0_, ...), custom_call_target="tpu_custom_call" | custom-call | flops 3750000128 | bytes 1 | tf_op jit(solution)/shard_map/pallas_call | solution.py:534
  317.4 8.6 %collective-permute-done.55 = bf16[32,5120]{1,0:T(8,128)(2,1)S(1)} collective-permute-done((bf16[32,5120]{1,0:T(8,128)(2,1)S(1)}, bf16[32,5120]{1,0:T(8,128)(2,1)S(1)}, u32[]{:S(2)}, u32[]{:S(2)}) %collective-permute-start.55) | collective-permute-done | bytes 327712 | tf_op jit(solution)/shard_map/ppermute | solution.py:68
  334.9 8.6 %collective-permute-done.58 = bf16[32,5120]{1,0:T(8,128)(2,1)S(1)} collective-permute-done((bf16[32,5120]{1,0:T(8,128)(2,1)S(1)}, bf16[32,5120]{1,0:T(8,128)(2,1)S(1)}, u32[]{:S(2)}, u32[]{:S(2)}) %collective-permute-start.58) | collective-permute-done | bytes 327712 | tf_op jit(solution)/shard_map/ppermute | solution.py:68
  351.1 11.1 %collective-permute-done.60 = bf16[32,3072]{1,0:T(8,128)(2,1)S(1)} collective-permute-done((bf16[32,3072]{1,0:T(8,128)(2,1)S(1)}, bf16[32,3072]{1,0:T(8,128)(2,1)S(1)}, u32[]{:S(2)}, u32[]{:S(2)}) %collective-permute-start.60) | collective-permute-done | bytes 196640 | tf_op jit(solution)/shard_map/ppermute | solution.py:68
  370.4 4.7 %collective-permute-done.63 = bf16[32,3072]{1,0:T(8,128)(2,1)S(1)} collective-permute-done((bf16[32,3072]{1,0:T(8,128)(2,1)S(1)}, bf16[32,3072]{1,0:T(8,128)(2,1)S(1)}, u32[]{:S(2)}, u32[]{:S(2)}) %collective-permute-start.63) | collective-permute-done | bytes 196640 | tf_op jit(solution)/shard_map/ppermute | solution.py:68
  (259 shorter events, 132.8 us)
Async XLA Ops:
  3.6 21.9 %collective-permute-start = (bf16[400,1024]{1,0:T(8,128)(2,1)}, bf16[400,1024]{1,0:T(8,128)(2,1)S(1)}, u32[]{:S(2)}, u32[]{:S(2)}) collective-permute-start(bf16[400,1024]{1,0:T(8,128)(2,1)} %shard_map.358.refs_0_), channel_id=1, source_target_pairs={{0,16},{4,12},{8,24},{12,4},{16,0},{20,28},{24,8},{28,20},{1,17},{... | collective-permute-start | bytes 2457608 | tf_op jit(solution)/shard_map/ppermute | solution.py:56
  6.6 18.9 %collective-permute-start.1 = (bf16[400,1024]{1,0:T(8,128)(2,1)}, bf16[400,1024]{1,0:T(8,128)(2,1)S(1)}, u32[]{:S(2)}, u32[]{:S(2)}) collective-permute-start(bf16[400,1024]{1,0:T(8,128)(2,1)} %shard_map.358.refs_0_), channel_id=1, source_target_pairs={{0,8},{4,20},{8,0},{12,28},{16,24},{20,4},{24,16},{28,12},{1,9},{5... | collective-permute-start | bytes 2457608 | tf_op jit(solution)/shard_map/ppermute | solution.py:56
  25.5 24.1 %collective-permute-start.6 = (bf16[128,4096]{1,0:T(8,128)(2,1)}, bf16[128,4096]{1,0:T(8,128)(2,1)}, u32[]{:S(2)}, u32[]{:S(2)}) collective-permute-start(bf16[128,4096]{1,0:T(8,128)(2,1)} %refs_0_.6), channel_id=1, source_target_pairs={{0,16},{4,12},{8,24},{12,4},{16,0},{20,28},{24,8},{28,20},{1,17},{... | collective-permute-start | bytes 3145736 | tf_op jit(solution)/shard_map/ppermute | solution.py:56
  27.9 20.7 %collective-permute-start.2 = (bf16[400,1024]{1,0:T(8,128)(2,1)S(1)}, bf16[400,1024]{1,0:T(8,128)(2,1)}, u32[]{:S(2)}, u32[]{:S(2)}) collective-permute-start(bf16[400,1024]{1,0:T(8,128)(2,1)S(1)} %collective-permute-done.refs_1_), channel_id=1, source_target_pairs={{0,8},{4,20},{8,0},{12,28},{16,24},{20,4},{24,16},{28,12},{1,9},{5... | collective-permute-start | bytes 2457608 | tf_op jit(solution)/shard_map/ppermute | solution.py:56
  28.6 20.0 %collective-permute-start.4 = (bf16[400,1024]{1,0:T(8,128)(2,1)S(1)}, bf16[400,1024]{1,0:T(8,128)(2,1)S(1)}, u32[]{:S(2)}, u32[]{:S(2)}) collective-permute-start(bf16[400,1024]{1,0:T(8,128)(2,1)S(1)} %collective-permute-done.refs_1_), channel_id=1, source_target_pairs={{0,4},{4,0},{8,12},{12,8},{16,20},{20,16},{24,28},{28,24},{1,5},{5... | collective-permute-start | bytes 2457608 | tf_op jit(solution)/shard_map/ppermute | solution.py:56
  28.6 20.0 %collective-permute-start.3 = (bf16[400,1024]{1,0:T(8,128)(2,1)S(1)}, bf16[400,1024]{1,0:T(8,128)(2,1)S(1)}, u32[]{:S(2)}, u32[]{:S(2)}) collective-permute-start(bf16[400,1024]{1,0:T(8,128)(2,1)S(1)} %copy-done.4), channel_id=1, source_target_pairs={{0,4},{4,0},{8,12},{12,8},{16,20},{20,16},{24,28},{28,24},{1,5},{5... | collective-permute-start | bytes 2457608 | tf_op jit(solution)/shard_map/ppermute | solution.py:56
  29.1 19.6 %collective-permute-start.5 = (bf16[400,1024]{1,0:T(8,128)(2,1)S(1)}, bf16[400,1024]{1,0:T(8,128)(2,1)S(1)}, u32[]{:S(2)}, u32[]{:S(2)}) collective-permute-start(bf16[400,1024]{1,0:T(8,128)(2,1)S(1)} %collective-permute-done.1.refs_2_), channel_id=1, source_target_pairs={{0,4},{4,0},{8,12},{12,8},{16,20},{20,16},{24,28},{28,24},{1,5},{5... | collective-permute-start | bytes 2457608 | tf_op jit(solution)/shard_map/ppermute | solution.py:56
  50.5 20.9 %collective-permute-start.8 = (bf16[128,4096]{1,0:T(8,128)(2,1)}, bf16[128,4096]{1,0:T(8,128)(2,1)}, u32[]{:S(2)}, u32[]{:S(2)}) collective-permute-start(bf16[128,4096]{1,0:T(8,128)(2,1)} %refs_0_.6), channel_id=1, source_target_pairs={{0,8},{4,20},{8,0},{12,28},{16,24},{20,4},{24,16},{28,12},{1,9},{5... | collective-permute-start | bytes 3145736 | tf_op jit(solution)/shard_map/ppermute | solution.py:56
  51.3 20.1 %collective-permute-start.10 = (bf16[128,1024]{1,0:T(8,128)(2,1)S(1)}, bf16[128,1024]{1,0:T(8,128)(2,1)}, u32[]{:S(2)}, u32[]{:S(2)}) collective-permute-start(bf16[128,1024]{1,0:T(8,128)(2,1)S(1)} %copy-done.25), channel_id=1, source_target_pairs={{0,8},{4,20},{8,0},{12,28},{16,24},{20,4},{24,16},{28,12},{1,9},{5... | collective-permute-start | bytes 786440 | tf_op jit(solution)/shard_map/ppermute | solution.py:56
  53.1 18.3 %collective-permute-start.9 = (bf16[128,1024]{1,0:T(8,128)(2,1)S(1)}, bf16[128,1024]{1,0:T(8,128)(2,1)}, u32[]{:S(2)}, u32[]{:S(2)}) collective-permute-start(bf16[128,1024]{1,0:T(8,128)(2,1)S(1)} %copy-done.25), channel_id=1, source_target_pairs={{0,16},{4,12},{8,24},{12,4},{16,0},{20,28},{24,8},{28,20},{1,17},{... | collective-permute-start | bytes 786440 | tf_op jit(solution)/shard_map/ppermute | solution.py:56
  71.4 17.2 %collective-permute-start.11 = (bf16[512,1024]{1,0:T(8,128)(2,1)S(1)}, bf16[512,1024]{1,0:T(8,128)(2,1)}, u32[]{:S(2)}, u32[]{:S(2)}) collective-permute-start(bf16[512,1024]{1,0:T(8,128)(2,1)S(1)} %copy-done), channel_id=1, source_target_pairs={{0,16},{4,12},{8,24},{12,4},{16,0},{20,28},{24,8},{28,20},{1,17},{... | collective-permute-start | bytes 3145736 | tf_op jit(solution)/shard_map/ppermute | solution.py:56
  91.2 25.4 %collective-permute-start.17 = (bf16[128,4096]{1,0:T(8,128)(2,1)}, bf16[128,4096]{1,0:T(8,128)(2,1)}, u32[]{:S(2)}, u32[]{:S(2)}) collective-permute-start(bf16[128,4096]{1,0:T(8,128)(2,1)} %collective-permute-done.6.refs_1_), channel_id=1, source_target_pairs={{0,8},{4,20},{8,0},{12,28},{16,24},{20,4},{24,16},{28,12},{1,9},{5... | collective-permute-start | bytes 3145736 | tf_op jit(solution)/shard_map/ppermute | solution.py:56
  92.5 24.1 %collective-permute-start.19 = (bf16[128,4096]{1,0:T(8,128)(2,1)}, bf16[128,4096]{1,0:T(8,128)(2,1)}, u32[]{:S(2)}, u32[]{:S(2)}) collective-permute-start(bf16[128,4096]{1,0:T(8,128)(2,1)} %collective-permute-done.6.refs_1_), channel_id=1, source_target_pairs={{0,4},{4,0},{8,12},{12,8},{16,20},{20,16},{24,28},{28,24},{1,5},{5... | collective-permute-start | bytes 3145736 | tf_op jit(solution)/shard_map/ppermute | solution.py:56
  92.6 24.1 %collective-permute-start.20 = (bf16[128,4096]{1,0:T(8,128)(2,1)}, bf16[128,4096]{1,0:T(8,128)(2,1)}, u32[]{:S(2)}, u32[]{:S(2)}) collective-permute-start(bf16[128,4096]{1,0:T(8,128)(2,1)} %collective-permute-done.8.refs_2_), channel_id=1, source_target_pairs={{0,4},{4,0},{8,12},{12,8},{16,20},{20,16},{24,28},{28,24},{1,5},{5... | collective-permute-start | bytes 3145736 | tf_op jit(solution)/shard_map/ppermute | solution.py:56
  178.2 26.4 %collective-permute-start.32 = (bf16[2,1024,512]{2,1,0:T(8,128)(2,1)}, bf16[2,1024,512]{2,1,0:T(8,128)(2,1)}, u32[]{:S(2)}, u32[]{:S(2)}) collective-permute-start(bf16[2,1024,512]{2,1,0:T(8,128)(2,1)} %get-tuple-element.352), channel_id=1, source_target_pairs={{0,8},{4,20},{8,0},{12,28},{16,24},{20,4},{24,16},{28,12},{1,9},{5... | collective-permute-start | bytes 6291464 | tf_op jit(solution)/shard_map/ppermute | solution.py:56
  209.0 20.7 %collective-permute-start.37 = (bf16[1024,512]{1,0:T(8,128)(2,1)}, bf16[1024,512]{1,0:T(8,128)(2,1)}, u32[]{:S(2)}, u32[]{:S(2)}) collective-permute-start(bf16[1024,512]{1,0:T(8,128)(2,1)} %get-tuple-element.540), channel_id=1, source_target_pairs={{0,16},{4,12},{8,24},{12,4},{16,0},{20,28},{24,8},{28,20},{1,17},{... | collective-permute-start | bytes 3145736 | tf_op jit(solution)/shard_map/ppermute | solution.py:56
  229.6 33.8 %collective-permute-start.40 = (bf16[2,128,5120]{2,1,0:T(8,128)(2,1)}, bf16[2,128,5120]{2,1,0:T(8,128)(2,1)}, u32[]{:S(2)}, u32[]{:S(2)}) collective-permute-start(bf16[2,128,5120]{2,1,0:T(8,128)(2,1)} %get-tuple-element.390), channel_id=1, source_target_pairs={{0,8},{4,20},{8,0},{12,28},{16,24},{20,4},{24,16},{28,12},{1,9},{5... | collective-permute-start | bytes 7864328 | tf_op jit(solution)/shard_map/ppermute | solution.py:56
  267.4 19.1 %collective-permute-start.45 = (bf16[128,5120]{1,0:T(8,128)(2,1)}, bf16[128,5120]{1,0:T(8,128)(2,1)}, u32[]{:S(2)}, u32[]{:S(2)}) collective-permute-start(bf16[128,5120]{1,0:T(8,128)(2,1)} %get-tuple-element.538), channel_id=1, source_target_pairs={{0,16},{4,12},{8,24},{12,4},{16,0},{20,28},{24,8},{28,20},{1,17},{... | collective-permute-start | bytes 3932168 | tf_op jit(solution)/shard_map/ppermute | solution.py:56
  286.5 20.7 %collective-permute-start.47 = (bf16[2,128,3072]{2,1,0:T(8,128)(2,1)}, bf16[2,128,3072]{2,1,0:T(8,128)(2,1)}, u32[]{:S(2)}, u32[]{:S(2)}) collective-permute-start(bf16[2,128,3072]{2,1,0:T(8,128)(2,1)} %get-tuple-element.438), channel_id=1, source_target_pairs={{0,8},{4,20},{8,0},{12,28},{16,24},{20,4},{24,16},{28,12},{1,9},{5... | collective-permute-start | bytes 4718600 | tf_op jit(solution)/shard_map/ppermute | solution.py:56
  290.4 16.7 %collective-permute-start.52 = (bf16[64,5120]{1,0:T(8,128)(2,1)}, bf16[64,5120]{1,0:T(8,128)(2,1)S(1)}, u32[]{:S(2)}, u32[]{:S(2)}) collective-permute-start(bf16[64,5120]{1,0:T(8,128)(2,1)} %get-tuple-element.549), channel_id=1, source_target_pairs={{0,1},{1,0},{2,3},{3,2},{4,5},{5,4},{6,7},{7,6},{8,9},{9,8},{10,11... | collective-permute-start | bytes 1966088 | tf_op jit(solution)/shard_map/ppermute | solution.py:68
  307.3 19.9 %collective-permute-start.56 = (bf16[512,512]{1,0:T(8,128)(2,1)S(1)}, bf16[512,512]{1,0:T(8,128)(2,1)S(1)}, u32[]{:S(2)}, u32[]{:S(2)}) collective-permute-start(bf16[512,512]{1,0:T(8,128)(2,1)S(1)} %pad_maximum_fusion.1), channel_id=1, source_target_pairs={{0,1},{1,0},{2,3},{3,2},{4,5},{5,4},{6,7},{7,6},{8,9},{9,8},{10,11... | collective-permute-start | bytes 1572872 | tf_op jit(solution)/shard_map/ppermute | solution.py:68
  310.2 16.9 %collective-permute-start.53 = (bf16[128,3072]{1,0:T(8,128)(2,1)S(1)}, bf16[128,3072]{1,0:T(8,128)(2,1)S(1)}, u32[]{:S(2)}, u32[]{:S(2)}) collective-permute-start(bf16[128,3072]{1,0:T(8,128)(2,1)S(1)} %get-tuple-element.542), channel_id=1, source_target_pairs={{0,16},{4,12},{8,24},{12,4},{16,0},{20,28},{24,8},{28,20},{1,17},{... | collective-permute-start | bytes 2359304 | tf_op jit(solution)/shard_map/ppermute | solution.py:56
  327.4 16.7 %collective-permute-start.57 = (bf16[64,3072]{1,0:T(8,128)(2,1)S(1)}, bf16[64,3072]{1,0:T(8,128)(2,1)S(1)}, u32[]{:S(2)}, u32[]{:S(2)}) collective-permute-start(bf16[64,3072]{1,0:T(8,128)(2,1)S(1)} %get-tuple-element.557), channel_id=1, source_target_pairs={{0,1},{1,0},{2,3},{3,2},{4,5},{5,4},{6,7},{7,6},{8,9},{9,8},{10,11... | collective-permute-start | bytes 1179656 | tf_op jit(solution)/shard_map/ppermute | solution.py:68
  346.0 17.9 %collective-permute-start.61 = (bf16[64,5120]{1,0:T(8,128)(2,1)S(1)}, bf16[64,5120]{1,0:T(8,128)(2,1)S(1)}, u32[]{:S(2)}, u32[]{:S(2)}) collective-permute-start(bf16[64,5120]{1,0:T(8,128)(2,1)S(1)} %pad_maximum_fusion), channel_id=1, source_target_pairs={{0,1},{1,0},{2,3},{3,2},{4,5},{5,4},{6,7},{7,6},{8,9},{9,8},{10,11... | collective-permute-start | bytes 1966088 | tf_op jit(solution)/shard_map/ppermute | solution.py:68
  (77 other events, 690.9 us)

commit v2 on v1

--- a/solution.py
+++ b/solution.py
@@ -19,7 +19,7 @@
 BF = jnp.bfloat16
 F32 = jnp.float32
 VMEM_LIMIT = 62 * 1024 * 1024
-SCALE = 0.3
+SCALE = 0.2
 
 
 def cost(microseconds):
@@ -243,6 +243,22 @@
         *[right for _, right in pairs],
         *others,
     )
+
+
+def upright_kernel(turned_ref, out_ref):
+    out_ref[...] = turned_ref[...].T.astype(F32)
+
+
+def upright(turned):
+    near = pl.BlockSpec(memory_space=pltpu.VMEM)
+    return pl.pallas_call(
+        upright_kernel,
+        out_shape=jax.ShapeDtypeStruct(turned.shape[::-1], F32),
+        in_specs=[near],
+        out_specs=near,
+        compiler_params=pltpu.CompilerParams(vmem_limit_bytes=VMEM_LIMIT),
+        cost_estimate=cost(3),
+    )(turned)
 
 
 def to_twin(blocks):
@@ -1396,7 +1412,7 @@
         other1 = trade(kept1, 1)
         small = small[0] + small_other
         small_other = trade(small, 1)
-        outer_own = paste(kept2, other2, 1).T.astype(F32)
+        outer_own = upright(paste(kept2, other2, 1))
         kept, other, kept1, other1, small, small_other, outer_own = phase(
             (kept, other, kept1, other1, small, small_other, outer_own)
         )

time: 393 us -> 393 us (level)
    unnamed x71 -> x72, local copies, waits for them, and re-layouts: 7.99 us -> 6.68 us
  transfers between devices with their start and end apart: 66 -> 66, of which waited for: 26 -> 26; matrix products, arithmetic and copies ran while one was open for 7% -> 6% of each run, Pallas kernels for 40% -> 41%
where the time goes in v2:
time: 393 us; the launch traced here: 387 us
  Pallas kernels  190 us (48%)
  waiting for transfers between devices  105 us (27%)
  starting transfers between devices  51.2 us (13%)
  other arithmetic  19.7 us (5%)
  local copies, waits for them, and re-layouts  13.1 us (3%)
  matrix products  5.96 us (2%)
    pallas_call x8, Pallas kernels, run(): pl.pallas_call(kernel, out_shape=tuple((jax.ShapeDtypeStruct(item[0], ite...  92.1 us
    ppermute x52, waiting for transfers between devices, hop(): return lax.ppermute(value, 'fsdp', pairs)  56.4 us
    ppermute x14, waiting for transfers between devices, trade(): return lax.ppermute(value, 'dp', [(i, i ^ bit) for i in range(4)])  49.1 us
    pallas_call x4, Pallas kernels, grad_blocks(): pl.pallas_call(partial(grad_kernel, first, tuple(counts), fold), grid_spe...  40.5 us
    ppermute x52, starting transfers between devices, hop(): return lax.ppermute(value, 'fsdp', pairs)  31 us
    ppermute x14, starting transfers between devices, trade(): return lax.ppermute(value, 'dp', [(i, i ^ bit) for i in range(4)])  20.2 us
    pallas_call x2, Pallas kernels, turned_blocks(): pl.pallas_call(partial(turned_kernel, first, fold), out_shape=shapes, in_...  15.4 us
    pallas_call x1, Pallas kernels, attend_back(): pl.pallas_call(attend_back_kernel, grid=(PAGES,), in_specs=[wide, wide, w...  14.7 us
  transfers between devices with their start and end apart: 66, of which 26 were waited for; matrix products, arithmetic and copies ran while one was open for 6% of the time, Pallas kernels for 41%

profile of v2, /device:TPU:0, one launch (start us, length us, event | category | flops | bytes accessed | tf_op | source)
XLA Modules:
  0.0 386.7 jit_solution(13921731677508222904)
XLA Ops:
  17.7 7.7 %collective-permute-done.refs_1_ = bf16[400,1024]{1,0:T(8,128)(2,1)S(1)} collective-permute-done((bf16[400,1024]{1,0:T(8,128)(2,1)}, bf16[400,1024]{1,0:T(8,128)(2,1)S(1)}, u32[]{:S(2)}, u32[]{:S(2)}) %collective-permute-start) | collective-permute-done | bytes 819232 | tf_op jit(solution)/shard_map/ppermute | solution.py:56
  29.1 19.5 %collective-permute-done.2.refs_3_ = bf16[400,1024]{1,0:T(8,128)(2,1)} collective-permute-done((bf16[400,1024]{1,0:T(8,128)(2,1)S(1)}, bf16[400,1024]{1,0:T(8,128)(2,1)}, u32[]{:S(2)}, u32[]{:S(2)}) %collective-permute-start.2) | collective-permute-done | bytes 819232 | tf_op jit(solution)/shard_map/ppermute | solution.py:56
  54.6 13.0 %shard_map.359 = (bf16[1024,1024]{1,0:T(8,128)(2,1)}, bf16[1024,1024]{1,0:T(8,128)(2,1)}, bf16[1024,1024]{1,0:T(8,128)(2,1)}, f32[16,4096]{1,0:T(8,128)}, f32[48,1,128]{2,1,0:T(1,128)}) custom-call(s32[8]{0:T(128)} %fusion.19.order_ref, bf16[1024,1024]{1,0:T(8,128)(2,1)} %fusion.5.x_ref.refs_0_, bf16[400,1024]{1,0:T(8,128)(2,1)} %shard_map.358.refs_0_, ...), custom_call_target="tpu_custom_call" | custom-call | flops 2400000000 | bytes 1 | tf_op jit(solution)/shard_map/pallas_call | solution.py:550
  73.3 14.6 %shard_map.361 = (bf16[1024,1024]{1,0:T(8,128)(2,1)}, bf16[8,8,128,256]{3,2,1,0:T(8,128)(2,1)}) custom-call(s32[8]{0:T(128)} %get-tuple-element.500.length_ref, bf16[1024,1024]{1,0:T(8,128)(2,1)} %get-tuple-element.278.q_ref, bf16[1024,1024]{1,0:T(8,128)(2,1)} %get-tuple-element.279.k_ref, bf16[1024,1024]{1,0:T(8,128)(2,1)} %get-tuple-element.280.v_ref, ...), custom_call_target="tpu_custom_call" | custom-call | flops 2700000000 | bytes 1 | tf_op jit(solution)/shard_map/pallas_call | solution.py:368
  93.4 9.0 %shard_map.362 = (bf16[544,1024]{1,0:T(8,128)(2,1)}, f32[544,1024]{1,0:T(8,128)}, f32[544,1]{1,0:T(8,128)}, bf16[544,1024]{1,0:T(8,128)(2,1)}) custom-call(s32[8]{0:T(128)} %fusion.19.order_ref, bf16[1024,1024]{1,0:T(8,128)(2,1)} %get-tuple-element.290.c_ref, bf16[544,1024]{1,0:T(8,128)(2,1)} %fusion.4.spread_ref, bf16[544,1024]{1,0:T(8,128)(2,1)} %hidden_ref.1, ...), custom_call_target="tpu_custom_call" | custom-call | flops 1400000000 | bytes 1 | tf_op jit(solution)/shard_map/pallas_call | solution.py:550
  104.9 11.2 %collective-permute-done.17.refs_3_ = bf16[128,4096]{1,0:T(8,128)(2,1)} collective-permute-done((bf16[128,4096]{1,0:T(8,128)(2,1)}, bf16[128,4096]{1,0:T(8,128)(2,1)}, u32[]{:S(2)}, u32[]{:S(2)}) %collective-permute-start.17) | collective-permute-done | bytes 1048608 | tf_op jit(solution)/shard_map/ppermute | solution.py:56
  119.9 12.4 %shard_map.363 = (bf16[544,4096]{1,0:T(8,128)(2,1)}, bf16[544,4096]{1,0:T(8,128)(2,1)}) custom-call(s32[8]{0:T(128)} %fusion.19.order_ref, bf16[544,1024]{1,0:T(8,128)(2,1)} %get-tuple-element.300.x_ref.refs_0_, f32[16,4096]{1,0:T(8,128)} %get-tuple-element.268.vector_ref, bf16[128,4096]{1,0:T(8,128)(2,1)} %refs_0_.6, ...), custom_call_target="tpu_custom_call" | custom-call | flops 2800000000 | bytes 1 | tf_op jit(solution)/shard_map/pallas_call | solution.py:550
  136.2 13.2 %shard_map.364 = (bf16[544,1024]{1,0:T(8,128)(2,1)}, f32[544,1024]{1,0:T(8,128)}, bf16[544,1024]{1,0:T(8,128)(2,1)}, f32[8,1024]{1,0:T(8,128)}) custom-call(s32[8]{0:T(128)} %fusion.19.order_ref, f32[16,4096]{1,0:T(8,128)} %get-tuple-element.268.vector_ref, bf16[544,4096]{1,0:T(8,128)(2,1)} %get-tuple-element.311.a_far.left_far, ...), custom_call_target="tpu_custom_call" | custom-call | flops 2300000000 | bytes 1 | tf_op jit(solution)/shard_map/pallas_call | solution.py:550
  149.4 7.3 %shard_map.365 = (bf16[1024,512]{1,0:T(8,128)(2,1)}, bf16[1024,512]{1,0:T(8,128)(2,1)}, bf16[1024,512]{1,0:T(8,128)(2,1)}, bf16[1024,512]{1,0:T(8,128)(2,1)}) custom-call(s32[8]{0:T(128)} %fusion.19.order_ref, bf16[544,1024]{1,0:T(8,128)(2,1)} %get-tuple-element.326.right_ref.d_ref, bf16[544,4096]{1,0:T(8,128)(2,1)} %get-tuple-element.311.a_far.left_far), custom_call_target="tpu_custom_call" | custom-call | flops 1400000000 | bytes 1 | tf_op jit(solution)/shard_map/pallas_call | solution.py:157
  157.8 10.8 %shard_map.366 = (bf16[544,4096]{1,0:T(8,128)(2,1)}, f32[8,4096]{1,0:T(8,128)}) custom-call(s32[8]{0:T(128)} %fusion.19.order_ref, bf16[544,1024]{1,0:T(8,128)(2,1)} %get-tuple-element.326.right_ref.d_ref, bf16[544,4096]{1,0:T(8,128)(2,1)} %get-tuple-element.327.steep_far, bf16[512,1024]{1,0:T(8,128)(2,1)} %refs_0_.5, ...), custom_call_target="tpu_custom_call" | custom-call | flops 2000000000 | bytes 1 | tf_op jit(solution)/shard_map/pallas_call | solution.py:550
  169.5 8.1 %shard_map.367 = (bf16[2,1024,512]{2,1,0:T(8,128)(2,1)}, bf16[2,1024,512]{2,1,0:T(8,128)(2,1)}) custom-call(s32[8]{0:T(128)} %fusion.19.order_ref, bf16[544,1024]{1,0:T(8,128)(2,1)} %get-tuple-element.326.right_ref.d_ref, bf16[544,4096]{1,0:T(8,128)(2,1)} %get-tuple-element.311.a_far.left_far, bf16[1024,512]{1,0:T(8,128)(2,1)} %copy-done.4, ...), custom_call_target="tpu_custom_call" | custom-call | flops 1400000000 | bytes 1 | tf_op jit(solution)/shard_map/pallas_call | solution.py:157
  178.9 12.9 %shard_map.368 = (f32[544,1024]{1,0:T(8,128)}, bf16[544,1024]{1,0:T(8,128)(2,1)}, f32[8,1024]{1,0:T(8,128)}) custom-call(s32[8]{0:T(128)} %fusion.19.order_ref, bf16[544,4096]{1,0:T(8,128)(2,1)} %get-tuple-element.342.d_ref.refs_2_, f32[544,1]{1,0:T(8,128)} %get-tuple-element.343.deviation_ref, f32[16,4096]{1,0:T(8,128)} %get-tuple-element.268.vector_ref, ...), custom_call_target="tpu_custom_call" | custom-call | flops 3200000000 | bytes 1 | tf_op jit(solution)/shard_map/pallas_call | solution.py:550
  191.8 10.7 %shard_map.369 = (bf16[128,5120]{1,0:T(8,128)(2,1)}, bf16[128,5120]{1,0:T(8,128)(2,1)}, bf16[128,5120]{1,0:T(8,128)(2,1)}, bf16[128,5120]{1,0:T(8,128)(2,1)}) custom-call(s32[8]{0:T(128)} %fusion.19.order_ref, bf16[544,1024]{1,0:T(8,128)(2,1)} %get-tuple-element.300.x_ref.refs_0_, bf16[544,1024]{1,0:T(8,128)(2,1)} %get-tuple-element.346.refs_1_, ...), custom_call_target="tpu_custom_call" | custom-call | flops 2000000000 | bytes 1 | tf_op jit(solution)/shard_map/pallas_call | solution.py:228
  209.6 8.5 %shard_map.370.g_ref = bf16[1024,1024]{1,0:T(8,128)(2,1)} custom-call(s32[8]{0:T(128)} %fusion.19.order_ref, bf16[544,1024]{1,0:T(8,128)(2,1)} %get-tuple-element.353.refs_3_.d_ref, bf16[1024,544]{1,0:T(8,128)(2,1)} %fusion.spread_ref, bf16[128,1024]{1,0:T(8,128)(2,1)} %refs_0_.7, bf16[128,1024]{1,0:T(8,128)(2,1)} %copy-done.7, bf16[128,1024]{1,0:T(8,128)(2,1)} %copy-done.6, ...), custom_call_target="tpu_custom_call" | custom-call | flops 1300000000 | bytes 1 | tf_op jit(solution)/shard_map/pallas_call | solution.py:550
  218.1 11.4 %shard_map.371 = (bf16[2,128,5120]{2,1,0:T(8,128)(2,1)}, bf16[2,128,5120]{2,1,0:T(8,128)(2,1)}) custom-call(s32[8]{0:T(128)} %fusion.19.order_ref, bf16[544,1024]{1,0:T(8,128)(2,1)} %get-tuple-element.300.x_ref.refs_0_, bf16[544,1024]{1,0:T(8,128)(2,1)} %get-tuple-element.346.refs_1_, bf16[544,4096]{1,0:T(8,128)(2,1)} %get-tuple-element.342.d_ref.refs_2_, ...), custom_call_target="tpu_custom_call" | custom-call | flops 2000000000 | bytes 1 | tf_op jit(solution)/shard_map/pallas_call | solution.py:228
  234.2 14.7 %shard_map.372 = (bf16[1024,3072]{1,0:T(8,128)(2,1)}, f32[16,256]{1,0:T(8,128)}, f32[2,16,128]{2,1,0:T(8,128)}, f32[8,3072]{1,0:T(8,128)}) custom-call(bf16[1024,1024]{1,0:T(8,128)(2,1)} %get-tuple-element.278.q_ref, bf16[1024,1024]{1,0:T(8,128)(2,1)} %get-tuple-element.279.k_ref, bf16[1024,1024]{1,0:T(8,128)(2,1)} %get-tuple-element.280.v_ref, ...), custom_call_target="tpu_custom_call" | custom-call | flops 2800000000 | bytes 1 | tf_op jit(solution)/shard_map/pallas_call | solution.py:479
  251.8 8.7 %shard_map.373 = (bf16[128,3072]{1,0:T(8,128)(2,1)}, bf16[128,3072]{1,0:T(8,128)(2,1)}, bf16[128,3072]{1,0:T(8,128)(2,1)}, bf16[128,3072]{1,0:T(8,128)(2,1)}) custom-call(s32[8]{0:T(128)} %fusion.19.order_ref, bf16[1024,1024]{1,0:T(8,128)(2,1)} %fusion.5.x_ref.refs_0_, bf16[1024,3072]{1,0:T(8,128)(2,1)} %get-tuple-element.439.refs_1_.d_ref), custom_call_target="tpu_custom_call" | custom-call | flops 1200000000 | bytes 1 | tf_op jit(solution)/shard_map/pallas_call | solution.py:228
  275.9 9.7 %shard_map.375 = (bf16[2,128,3072]{2,1,0:T(8,128)(2,1)}, bf16[2,128,3072]{2,1,0:T(8,128)(2,1)}) custom-call(s32[8]{0:T(128)} %fusion.19.order_ref, bf16[1024,1024]{1,0:T(8,128)(2,1)} %fusion.5.x_ref.refs_0_, bf16[1024,3072]{1,0:T(8,128)(2,1)} %get-tuple-element.439.refs_1_.d_ref, bf16[128,3072]{1,0:T(8,128)(2,1)} %collective-permute-done.41.refs_2_, ...), custom_call_target="tpu_custom_call" | custom-call | flops 1200000000 | bytes 1 | tf_op jit(solution)/shard_map/pallas_call | solution.py:228
  292.4 12.4 %shard_map.376 = f32[544,1024]{1,0:T(8,128)} custom-call(s32[8]{0:T(128)} %fusion.19.order_ref, bf16[1024,3072]{1,0:T(8,128)(2,1)} %get-tuple-element.439.refs_1_.d_ref, bf16[544,1024]{1,0:T(8,128)(2,1)} %fusion.4.spread_ref, f32[544,1024]{1,0:T(8,128)} %get-tuple-element.440.summed_far, bf16[400,1024]{1,0:T(8,128)(2,1)} %shard_map.358.refs_0_, ...), custom_call_target="tpu_custom_call" | custom-call | flops 2500000000 | bytes 1 | tf_op jit(solution)/shard_map/pallas_call | solution.py:550
  317.0 8.8 %collective-permute-done.55 = bf16[32,5120]{1,0:T(8,128)(2,1)S(1)} collective-permute-done((bf16[32,5120]{1,0:T(8,128)(2,1)S(1)}, bf16[32,5120]{1,0:T(8,128)(2,1)S(1)}, u32[]{:S(2)}, u32[]{:S(2)}) %collective-permute-start.55) | collective-permute-done | bytes 327712 | tf_op jit(solution)/shard_map/ppermute | solution.py:68
  334.8 8.5 %collective-permute-done.58 = bf16[32,5120]{1,0:T(8,128)(2,1)S(1)} collective-permute-done((bf16[32,5120]{1,0:T(8,128)(2,1)S(1)}, bf16[32,5120]{1,0:T(8,128)(2,1)S(1)}, u32[]{:S(2)}, u32[]{:S(2)}) %collective-permute-start.58) | collective-permute-done | bytes 327712 | tf_op jit(solution)/shard_map/ppermute | solution.py:68
  353.1 9.5 %collective-permute-done.60 = bf16[32,3072]{1,0:T(8,128)(2,1)S(1)} collective-permute-done((bf16[32,3072]{1,0:T(8,128)(2,1)S(1)}, bf16[32,3072]{1,0:T(8,128)(2,1)S(1)}, u32[]{:S(2)}, u32[]{:S(2)}) %collective-permute-start.60) | collective-permute-done | bytes 196640 | tf_op jit(solution)/shard_map/ppermute | solution.py:68
  370.6 4.3 %collective-permute-done.63 = bf16[32,3072]{1,0:T(8,128)(2,1)S(1)} collective-permute-done((bf16[32,3072]{1,0:T(8,128)(2,1)S(1)}, bf16[32,3072]{1,0:T(8,128)(2,1)S(1)}, u32[]{:S(2)}, u32[]{:S(2)}) %collective-permute-start.63) | collective-permute-done | bytes 196640 | tf_op jit(solution)/shard_map/ppermute | solution.py:68
  377.5 6.0 %collective-permute-done.65 = bf16[64,3072]{1,0:T(8,128)(2,1)S(1)} collective-permute-done((bf16[64,3072]{1,0:T(8,128)(2,1)S(1)}, bf16[64,3072]{1,0:T(8,128)(2,1)S(1)}, u32[]{:S(2)}, u32[]{:S(2)}) %collective-permute-start.65) | collective-permute-done | bytes 393248 | tf_op jit(solution)/shard_map/ppermute | solution.py:68
  (261 shorter events, 132.3 us)
Async XLA Ops:
  3.6 21.9 %collective-permute-start = (bf16[400,1024]{1,0:T(8,128)(2,1)}, bf16[400,1024]{1,0:T(8,128)(2,1)S(1)}, u32[]{:S(2)}, u32[]{:S(2)}) collective-permute-start(bf16[400,1024]{1,0:T(8,128)(2,1)} %shard_map.358.refs_0_), channel_id=1, source_target_pairs={{0,16},{4,12},{8,24},{12,4},{16,0},{20,28},{24,8},{28,20},{1,17},{... | collective-permute-start | bytes 2457608 | tf_op jit(solution)/shard_map/ppermute | solution.py:56
  6.6 18.9 %collective-permute-start.1 = (bf16[400,1024]{1,0:T(8,128)(2,1)}, bf16[400,1024]{1,0:T(8,128)(2,1)S(1)}, u32[]{:S(2)}, u32[]{:S(2)}) collective-permute-start(bf16[400,1024]{1,0:T(8,128)(2,1)} %shard_map.358.refs_0_), channel_id=1, source_target_pairs={{0,8},{4,20},{8,0},{12,28},{16,24},{20,4},{24,16},{28,12},{1,9},{5... | collective-permute-start | bytes 2457608 | tf_op jit(solution)/shard_map/ppermute | solution.py:56
  25.5 24.1 %collective-permute-start.6 = (bf16[128,4096]{1,0:T(8,128)(2,1)}, bf16[128,4096]{1,0:T(8,128)(2,1)}, u32[]{:S(2)}, u32[]{:S(2)}) collective-permute-start(bf16[128,4096]{1,0:T(8,128)(2,1)} %refs_0_.6), channel_id=1, source_target_pairs={{0,16},{4,12},{8,24},{12,4},{16,0},{20,28},{24,8},{28,20},{1,17},{... | collective-permute-start | bytes 3145736 | tf_op jit(solution)/shard_map/ppermute | solution.py:56
  27.9 20.7 %collective-permute-start.2 = (bf16[400,1024]{1,0:T(8,128)(2,1)S(1)}, bf16[400,1024]{1,0:T(8,128)(2,1)}, u32[]{:S(2)}, u32[]{:S(2)}) collective-permute-start(bf16[400,1024]{1,0:T(8,128)(2,1)S(1)} %collective-permute-done.refs_1_), channel_id=1, source_target_pairs={{0,8},{4,20},{8,0},{12,28},{16,24},{20,4},{24,16},{28,12},{1,9},{5... | collective-permute-start | bytes 2457608 | tf_op jit(solution)/shard_map/ppermute | solution.py:56
  28.6 20.0 %collective-permute-start.4 = (bf16[400,1024]{1,0:T(8,128)(2,1)S(1)}, bf16[400,1024]{1,0:T(8,128)(2,1)S(1)}, u32[]{:S(2)}, u32[]{:S(2)}) collective-permute-start(bf16[400,1024]{1,0:T(8,128)(2,1)S(1)} %collective-permute-done.refs_1_), channel_id=1, source_target_pairs={{0,4},{4,0},{8,12},{12,8},{16,20},{20,16},{24,28},{28,24},{1,5},{5... | collective-permute-start | bytes 2457608 | tf_op jit(solution)/shard_map/ppermute | solution.py:56
  28.6 20.0 %collective-permute-start.3 = (bf16[400,1024]{1,0:T(8,128)(2,1)S(1)}, bf16[400,1024]{1,0:T(8,128)(2,1)S(1)}, u32[]{:S(2)}, u32[]{:S(2)}) collective-permute-start(bf16[400,1024]{1,0:T(8,128)(2,1)S(1)} %copy-done.12), channel_id=1, source_target_pairs={{0,4},{4,0},{8,12},{12,8},{16,20},{20,16},{24,28},{28,24},{1,5},{5... | collective-permute-start | bytes 2457608 | tf_op jit(solution)/shard_map/ppermute | solution.py:56
  29.1 19.6 %collective-permute-start.5 = (bf16[400,1024]{1,0:T(8,128)(2,1)S(1)}, bf16[400,1024]{1,0:T(8,128)(2,1)S(1)}, u32[]{:S(2)}, u32[]{:S(2)}) collective-permute-start(bf16[400,1024]{1,0:T(8,128)(2,1)S(1)} %collective-permute-done.1.refs_2_), channel_id=1, source_target_pairs={{0,4},{4,0},{8,12},{12,8},{16,20},{20,16},{24,28},{28,24},{1,5},{5... | collective-permute-start | bytes 2457608 | tf_op jit(solution)/shard_map/ppermute | solution.py:56
  50.5 20.9 %collective-permute-start.8 = (bf16[128,4096]{1,0:T(8,128)(2,1)}, bf16[128,4096]{1,0:T(8,128)(2,1)}, u32[]{:S(2)}, u32[]{:S(2)}) collective-permute-start(bf16[128,4096]{1,0:T(8,128)(2,1)} %refs_0_.6), channel_id=1, source_target_pairs={{0,8},{4,20},{8,0},{12,28},{16,24},{20,4},{24,16},{28,12},{1,9},{5... | collective-permute-start | bytes 3145736 | tf_op jit(solution)/shard_map/ppermute | solution.py:56
  51.3 20.1 %collective-permute-start.10 = (bf16[128,1024]{1,0:T(8,128)(2,1)S(1)}, bf16[128,1024]{1,0:T(8,128)(2,1)S(1)}, u32[]{:S(2)}, u32[]{:S(2)}) collective-permute-start(bf16[128,1024]{1,0:T(8,128)(2,1)S(1)} %copy-done.5), channel_id=1, source_target_pairs={{0,8},{4,20},{8,0},{12,28},{16,24},{20,4},{24,16},{28,12},{1,9},{5... | collective-permute-start | bytes 786440 | tf_op jit(solution)/shard_map/ppermute | solution.py:56
  53.1 18.3 %collective-permute-start.9 = (bf16[128,1024]{1,0:T(8,128)(2,1)S(1)}, bf16[128,1024]{1,0:T(8,128)(2,1)S(1)}, u32[]{:S(2)}, u32[]{:S(2)}) collective-permute-start(bf16[128,1024]{1,0:T(8,128)(2,1)S(1)} %copy-done.5), channel_id=1, source_target_pairs={{0,16},{4,12},{8,24},{12,4},{16,0},{20,28},{24,8},{28,20},{1,17},{... | collective-permute-start | bytes 786440 | tf_op jit(solution)/shard_map/ppermute | solution.py:56
  71.4 17.0 %collective-permute-start.11 = (bf16[512,1024]{1,0:T(8,128)(2,1)S(1)}, bf16[512,1024]{1,0:T(8,128)(2,1)}, u32[]{:S(2)}, u32[]{:S(2)}) collective-permute-start(bf16[512,1024]{1,0:T(8,128)(2,1)S(1)} %copy-done), channel_id=1, source_target_pairs={{0,16},{4,12},{8,24},{12,4},{16,0},{20,28},{24,8},{28,20},{1,17},{... | collective-permute-start | bytes 3145736 | tf_op jit(solution)/shard_map/ppermute | solution.py:56
  91.2 24.9 %collective-permute-start.17 = (bf16[128,4096]{1,0:T(8,128)(2,1)}, bf16[128,4096]{1,0:T(8,128)(2,1)}, u32[]{:S(2)}, u32[]{:S(2)}) collective-permute-start(bf16[128,4096]{1,0:T(8,128)(2,1)} %collective-permute-done.6.refs_1_), channel_id=1, source_target_pairs={{0,8},{4,20},{8,0},{12,28},{16,24},{20,4},{24,16},{28,12},{1,9},{5... | collective-permute-start | bytes 3145736 | tf_op jit(solution)/shard_map/ppermute | solution.py:56
  92.0 24.1 %collective-permute-start.19 = (bf16[128,4096]{1,0:T(8,128)(2,1)}, bf16[128,4096]{1,0:T(8,128)(2,1)}, u32[]{:S(2)}, u32[]{:S(2)}) collective-permute-start(bf16[128,4096]{1,0:T(8,128)(2,1)} %collective-permute-done.6.refs_1_), channel_id=1, source_target_pairs={{0,4},{4,0},{8,12},{12,8},{16,20},{20,16},{24,28},{28,24},{1,5},{5... | collective-permute-start | bytes 3145736 | tf_op jit(solution)/shard_map/ppermute | solution.py:56
  92.7 23.4 %collective-permute-start.20 = (bf16[128,4096]{1,0:T(8,128)(2,1)}, bf16[128,4096]{1,0:T(8,128)(2,1)}, u32[]{:S(2)}, u32[]{:S(2)}) collective-permute-start(bf16[128,4096]{1,0:T(8,128)(2,1)} %collective-permute-done.8.refs_2_), channel_id=1, source_target_pairs={{0,4},{4,0},{8,12},{12,8},{16,20},{20,16},{24,28},{28,24},{1,5},{5... | collective-permute-start | bytes 3145736 | tf_op jit(solution)/shard_map/ppermute | solution.py:56
  177.6 26.4 %collective-permute-start.32 = (bf16[2,1024,512]{2,1,0:T(8,128)(2,1)}, bf16[2,1024,512]{2,1,0:T(8,128)(2,1)}, u32[]{:S(2)}, u32[]{:S(2)}) collective-permute-start(bf16[2,1024,512]{2,1,0:T(8,128)(2,1)} %get-tuple-element.352), channel_id=1, source_target_pairs={{0,8},{4,20},{8,0},{12,28},{16,24},{20,4},{24,16},{28,12},{1,9},{5... | collective-permute-start | bytes 6291464 | tf_op jit(solution)/shard_map/ppermute | solution.py:56
  208.4 21.1 %collective-permute-start.37 = (bf16[1024,512]{1,0:T(8,128)(2,1)}, bf16[1024,512]{1,0:T(8,128)(2,1)}, u32[]{:S(2)}, u32[]{:S(2)}) collective-permute-start(bf16[1024,512]{1,0:T(8,128)(2,1)} %get-tuple-element.504), channel_id=1, source_target_pairs={{0,16},{4,12},{8,24},{12,4},{16,0},{20,28},{24,8},{28,20},{1,17},{... | collective-permute-start | bytes 3145736 | tf_op jit(solution)/shard_map/ppermute | solution.py:56
  229.5 33.4 %collective-permute-start.40 = (bf16[2,128,5120]{2,1,0:T(8,128)(2,1)}, bf16[2,128,5120]{2,1,0:T(8,128)(2,1)}, u32[]{:S(2)}, u32[]{:S(2)}) collective-permute-start(bf16[2,128,5120]{2,1,0:T(8,128)(2,1)} %get-tuple-element.390), channel_id=1, source_target_pairs={{0,8},{4,20},{8,0},{12,28},{16,24},{20,4},{24,16},{28,12},{1,9},{5... | collective-permute-start | bytes 7864328 | tf_op jit(solution)/shard_map/ppermute | solution.py:56
  232.5 16.4 %collective-permute-start.38 = (bf16[512,512]{1,0:T(8,128)(2,1)S(1)}, bf16[512,512]{1,0:T(8,128)(2,1)S(1)}, u32[]{:S(2)}, u32[]{:S(2)}) collective-permute-start(bf16[512,512]{1,0:T(8,128)(2,1)S(1)} %get-tuple-element.517), channel_id=1, source_target_pairs={{0,1},{1,0},{2,3},{3,2},{4,5},{5,4},{6,7},{7,6},{8,9},{9,8},{10,11... | collective-permute-start | bytes 1572872 | tf_op jit(solution)/shard_map/ppermute | solution.py:68
  266.8 19.5 %collective-permute-start.45 = (bf16[128,5120]{1,0:T(8,128)(2,1)}, bf16[128,5120]{1,0:T(8,128)(2,1)}, u32[]{:S(2)}, u32[]{:S(2)}) collective-permute-start(bf16[128,5120]{1,0:T(8,128)(2,1)} %get-tuple-element.502), channel_id=1, source_target_pairs={{0,16},{4,12},{8,24},{12,4},{16,0},{20,28},{24,8},{28,20},{1,17},{... | collective-permute-start | bytes 3932168 | tf_op jit(solution)/shard_map/ppermute | solution.py:56
  286.4 20.7 %collective-permute-start.47 = (bf16[2,128,3072]{2,1,0:T(8,128)(2,1)}, bf16[2,128,3072]{2,1,0:T(8,128)(2,1)}, u32[]{:S(2)}, u32[]{:S(2)}) collective-permute-start(bf16[2,128,3072]{2,1,0:T(8,128)(2,1)} %get-tuple-element.438), channel_id=1, source_target_pairs={{0,8},{4,20},{8,0},{12,28},{16,24},{20,4},{24,16},{28,12},{1,9},{5... | collective-permute-start | bytes 4718600 | tf_op jit(solution)/shard_map/ppermute | solution.py:56
  289.8 16.6 %collective-permute-start.52 = (bf16[64,5120]{1,0:T(8,128)(2,1)}, bf16[64,5120]{1,0:T(8,128)(2,1)S(1)}, u32[]{:S(2)}, u32[]{:S(2)}) collective-permute-start(bf16[64,5120]{1,0:T(8,128)(2,1)} %get-tuple-element.513), channel_id=1, source_target_pairs={{0,1},{1,0},{2,3},{3,2},{4,5},{5,4},{6,7},{7,6},{8,9},{9,8},{10,11... | collective-permute-start | bytes 1966088 | tf_op jit(solution)/shard_map/ppermute | solution.py:68
  307.2 20.1 %collective-permute-start.56 = (bf16[512,512]{1,0:T(8,128)(2,1)S(1)}, bf16[512,512]{1,0:T(8,128)(2,1)S(1)}, u32[]{:S(2)}, u32[]{:S(2)}) collective-permute-start(bf16[512,512]{1,0:T(8,128)(2,1)S(1)} %pad_maximum_fusion.2), channel_id=1, source_target_pairs={{0,1},{1,0},{2,3},{3,2},{4,5},{5,4},{6,7},{7,6},{8,9},{9,8},{10,11... | collective-permute-start | bytes 1572872 | tf_op jit(solution)/shard_map/ppermute | solution.py:68
  310.0 17.3 %collective-permute-start.53 = (bf16[128,3072]{1,0:T(8,128)(2,1)S(1)}, bf16[128,3072]{1,0:T(8,128)(2,1)S(1)}, u32[]{:S(2)}, u32[]{:S(2)}) collective-permute-start(bf16[128,3072]{1,0:T(8,128)(2,1)S(1)} %get-tuple-element.506), channel_id=1, source_target_pairs={{0,16},{4,12},{8,24},{12,4},{16,0},{20,28},{24,8},{28,20},{1,17},{... | collective-permute-start | bytes 2359304 | tf_op jit(solution)/shard_map/ppermute | solution.py:56
  346.2 17.9 %collective-permute-start.61 = (bf16[64,5120]{1,0:T(8,128)(2,1)S(1)}, bf16[64,5120]{1,0:T(8,128)(2,1)S(1)}, u32[]{:S(2)}, u32[]{:S(2)}) collective-permute-start(bf16[64,5120]{1,0:T(8,128)(2,1)S(1)} %pad_maximum_fusion.1), channel_id=1, source_target_pairs={{0,1},{1,0},{2,3},{3,2},{4,5},{5,4},{6,7},{7,6},{8,9},{9,8},{10,11... | collective-permute-start | bytes 1966088 | tf_op jit(solution)/shard_map/ppermute | solution.py:68
  (78 other events, 714.6 us)
